TPU v7x, 32 devices: a whole 2x2x4 slice. The times are simulated.
32 devices in a mesh: pair: 4 (over x, core), pw: 8 (over z, y).
Axes of the slice: x: 2, y: 2, z: 4, core: 2. Of those that a mesh axis runs over, the one named last changes fastest.
Arguments:
- pair_products: bfloat16 [32768, 2048], P('pw', 'pair'), may hold values from -40 to 40
- basis: bfloat16 [32768, 1024], P('pw'), may hold values from -0.046875 to 0.046875
- val_energy: float32 [128], replicated, may hold values from -0.05 to -0.001
- cond_energy: float32 [128], replicated, may hold values from 0.001 to 40
- frequencies: float32 [8], replicated, may hold values from 0.002 to 20
- valence_index: int32 [2048], P('pair'), may hold values from 0 to 127
- conduction_index: int32 [2048], P('pair'), may hold values from 0 to 127
Outputs:
- response: float32 [8, 1024, 1024], P(None, 'pw', 'pair')
All inputs are finite; a program needn't handle non-finite values.
Results may differ from a plain program's by a relative error of at most 0.0055.
Values may be sent and summed in bfloat16 or wider, within the bound.
No kernel may reach another device: no remote copies, remote signals or barrier semaphores. Data moves between devices by JAX's collectives and lax.ppermute only.
A program may use at most 64 MiB of HBM per device.

v0:
```python
import jax
import jax.numpy as jnp
from jax import lax
from jax.sharding import PartitionSpec as P

GROUPS = 2


def lookup(index_array, table):
    levels = lax.broadcasted_iota(jnp.int32, (index_array.shape[0], table.shape[0]), 1)
    return jnp.sum(jnp.where(index_array[:, None] == levels, table[None, :], 0.0), axis=1)


def make_weights(
    valence_index, conduction_index, val_energy, cond_energy, frequencies, pairs_total
):
    energy_gap = lookup(conduction_index, cond_energy) - lookup(valence_index, val_energy)
    return (
        -4.0
        * energy_gap[None, :]
        / (energy_gap[None, :] ** 2 + frequencies[:, None] ** 2)
        / pairs_total
    )


def scaled(weight_block, own_rows):
    return (weight_block[:, None, :] * own_rows.astype(jnp.float32)[None]).astype(jnp.bfloat16)


def per_device(
    pair_products, basis, val_energy, cond_energy, frequencies, valence_index, conduction_index
):
    rows_local = pair_products.shape[1]
    pairs_total = rows_local * lax.axis_size("pair")
    block_size = rows_local // GROUPS
    rows_own = basis.shape[1] // lax.axis_size("pw")
    weights = make_weights(
        valence_index, conduction_index, val_energy, cond_energy, frequencies, pairs_total
    )
    gram_total = None
    kept_rows = []
    for group in range(GROUPS):
        pair_block = pair_products[:, group * block_size : (group + 1) * block_size]
        weight_block = weights[:, group * block_size : (group + 1) * block_size]
        gram_rows = None
        partial_sums = lax.dot_general(
            basis, pair_block, (((0,), (0,)), ((), ())), preferred_element_type=jnp.float32
        )
        projected_all = lax.psum(partial_sums, "pw").astype(jnp.bfloat16)
        own_rows = lax.dynamic_slice_in_dim(
            projected_all, lax.axis_index("pw") * rows_own, rows_own, 0
        )
        weighted = scaled(weight_block, own_rows)
        gram_rows = jnp.einsum(
            "kpc,nc->kpn", weighted, projected_all, preferred_element_type=jnp.float32
        )
        kept_rows.append(own_rows)
        summed_part = lax.psum_scatter(gram_rows, "pair", scatter_dimension=2, tiled=True)
        gram_total = summed_part if gram_total is None else gram_total + summed_part
    return gram_total


def solution(mesh):
    placed = (P("pw", "pair"), P("pw", None), P(), P(), P(), P("pair"), P("pair"))
    return jax.shard_map(
        per_device, mesh=mesh, in_specs=placed, out_specs=P(None, "pw", "pair"), check_vma=False
    )
```

profile of v0, /device:TPU:0, one launch (start us, length us, event | category | flops | bytes accessed | tf_op | source)
XLA Modules:
  0.0 165.1 jit_solution(6754413563477947304)
XLA Ops:
  6.5 0.0 reduce-scatter.2.cloned.1.call-start
  6.5 0.0 copy-start.4
  6.5 6.5 %fusion = f32[1024,256]{1,0:T(8,128)S(1)} fusion(bf16[4096,1024]{1,0:T(8,128)(2,1)} %param.8, bf16[4096,512]{1,0:T(8,128)(2,1)} %param.7), kind=kOutput, calls=%fused_computation.1 | convolution fusion | flops 2147483648 | bytes 11534336 | tf_op jit(solution)/shard_map/dot_general | solution.py:46
  13.0 0.0 copy-done.4
  13.0 0.0 copy-start.5
  13.1 0.0 copy-start
  13.1 0.0 copy-start.1
  13.1 0.0 copy-start.2
  13.1 0.0 copy-start.3
  13.1 4.0 %fusion.2 = f32[1024,256]{1,0:T(8,128)S(1)} fusion(bf16[4096,1024]{1,0:T(8,128)(2,1)S(1)} %copy-done.4, bf16[4096,512]{1,0:T(8,128)(2,1)} %param.7), kind=kOutput, calls=%fused_computation.3 | convolution fusion | flops 2147483648 | bytes 11534336 | tf_op jit(solution)/shard_map/dot_general | solution.py:46
  17.1 0.0 copy-done.5
  17.1 0.0 copy-done
  17.1 0.0 copy-done.1
  17.2 0.0 copy-done.2
  17.2 0.0 copy-done.3
  17.2 0.4 select_reduce_fusion
  17.6 0.1 divide_multiply_fusion
  17.6 92.6 %all-reduce.2 = (bf16[1024,256]{1,0:T(8,128)(2,1)S(1)}, bf16[1024,256]{1,0:T(8,128)(2,1)S(1)}) all-reduce(f32[1024,256]{1,0:T(8,128)S(1)} %fusion.2, f32[1024,256]{1,0:T(8,128)S(1)} %fusion), channel_id=1, replica_groups=mesh['pair'=4,'pw'=8] {'pw'}, use_global_device_ids=true, to_apply=%region_2.3 | all-reduce | flops 524288 | bytes 3145728 | tf_op jit(solution)/shard_map/psum | solution.py:49
  110.3 0.7 fusion.4
  111.0 2.7 %convolution_add_fusion = f32[8,128,1024]{2,1,0:T(8,128)} fusion(f32[8,128,1024]{2,1,0:T(8,128)S(1)} %fusion.4, bf16[1024,256]{1,0:T(8,128)(2,1)S(1)} %get-tuple-element.6, f32[128,256]{1,0:T(8,128)S(1)} %get-tuple-element.11, f32[8,256]{1,0:T(8,128)S(1)} %get-tuple-element.7), kind=kOutput, calls=%fused_computation | convolution fusion | flops 538443776 | bytes 9052160 | tf_op jit(solution)/shard_map/kpc,nc->kpn/dot_general | solution.py:54
  113.7 0.0 reduce-scatter.2.cloned.1.call-update
  113.7 44.5 %reduce-scatter.2.cloned.1.call-done = f32[8,128,256]{2,1,0:T(8,128)} async-done(((f32[8,128,1024]{2,1,0:T(8,128)}), f32[8,128,256]{2,1,0:T(8,128)}) %reduce-scatter.2.cloned.1.call-update) | async-done | bytes 1048592 | tf_op jit(solution)/shard_map/reduce_scatter | solution.py:58
  (4 shorter events, 0.0 us)
Async XLA Ops:
  6.5 151.7 %reduce-scatter.2.cloned.1.call-start = ((), (), s32[]{:S(2)}) async-start(), calls=%async_computation.1 | async-start | bytes 5242880 | tf_op jit(solution)/shard_map/reduce_scatter | solution.py:58
  6.5 6.5 %copy-start.4 = (bf16[4096,1024]{1,0:T(8,128)(2,1)S(1)}, bf16[4096,1024]{1,0:T(8,128)(2,1)}, u32[]{:S(2)}) copy-start(bf16[4096,1024]{1,0:T(8,128)(2,1)} %param.8) | copy-start | bytes 25165828
  13.0 4.1 %copy-start.5 = (f32[8]{0:T(128)S(1)}, f32[8]{0:T(128)}, u32[]{:S(2)}) copy-start(f32[8]{0:T(128)} %param.11) | copy-start | bytes 100
  13.1 4.1 %copy-start = (s32[512]{0:T(512)S(1)}, s32[512]{0:T(512)}, u32[]{:S(2)}) copy-start(s32[512]{0:T(512)} %param.12) | copy-start | bytes 6148
  13.1 4.1 %copy-start.1 = (s32[512]{0:T(512)S(1)}, s32[512]{0:T(512)}, u32[]{:S(2)}) copy-start(s32[512]{0:T(512)} %param.13) | copy-start | bytes 6148
  13.1 4.1 %copy-start.2 = (f32[128]{0:T(128)S(1)}, f32[128]{0:T(128)}, u32[]{:S(2)}) copy-start(f32[128]{0:T(128)} %param.9) | copy-start | bytes 1540
  13.1 4.1 %copy-start.3 = (f32[128]{0:T(128)S(1)}, f32[128]{0:T(128)}, u32[]{:S(2)}) copy-start(f32[128]{0:T(128)} %param.10) | copy-start | bytes 1540
Sparse Core Ops, SparseCore 0:
  113.9 44.3 reduce-scatter.1
where the time goes:
time: 165 us
  blocking collectives  92.6 us (56%)
  waiting for transfers between devices  44.5 us (27%)
  matrix products  13.9 us (8%)
  between operations  13.5 us (8%)
    psum x1, blocking collectives, per_device(): projected_all = lax.psum(partial_sums, 'pw').astype(jnp.bfloat16)  92.6 us
    reduce_scatter x1, waiting for transfers between devices, per_device(): lax.psum_scatter(gram_rows, 'pair', scatter_dimension=2, tiled=True)  44.5 us
    dot_general x2, matrix products, per_device(): lax.dot_general(basis, pair_block, (((0,), (0,)), ((), ())), preferred_el...  10.5 us
    dot_general x2, matrix products, per_device(): jnp.einsum('kpc,nc->kpn', weighted, projected_all, preferred_element_type...  3.44 us
  transfers between devices with their start and end apart: 1, of which 1 were waited for; matrix products, arithmetic and copies ran while one was open for 0% of the time, Pallas kernels for 0%

commit v1 on v0

v1 whole, which is shorter than its diff:
```python
import jax
import jax.numpy as jnp
from jax import lax
from jax.sharding import PartitionSpec as P

GROUPS = 2
GAP_ROWS = 16


def lookup(index_array, table):
    levels = lax.broadcasted_iota(jnp.int32, (index_array.shape[0], table.shape[0]), 1)
    return jnp.sum(jnp.where(index_array[:, None] == levels, table[None, :], 0.0), axis=1)


def flip(size, mask):
    return [(i, i ^ mask) for i in range(size)]


def split_gap(gap):
    parts = []
    left = gap
    for _ in range(3):
        part = lax.reduce_precision(left, 8, 7)
        parts.append(part.astype(jnp.bfloat16))
        left = left - part
    rows = jnp.stack(parts)
    return jnp.pad(rows, ((0, GAP_ROWS - rows.shape[0]), (0, 0)))


def join_gap(rows):
    terms = rows[:3].astype(jnp.float32)
    return terms[0] + (terms[1] + terms[2])


def halves(blocks, bit, place):
    n, rows, cols = blocks.shape
    low = 1 << place
    view = blocks.reshape(n // (2 * low), 2, low, rows, cols)
    pick = lambda b: lax.dynamic_index_in_dim(view, b, 1, False).reshape(n // 2, rows, cols)
    return pick(bit), pick(1 - bit)


def merge(mine, other, bit, place):
    n, rows, cols = mine.shape
    low = 1 << place
    first = jnp.where(bit == 0, mine, other).reshape(n // low, 1, low, rows, cols)
    second = jnp.where(bit == 0, other, mine).reshape(n // low, 1, low, rows, cols)
    return jnp.concatenate([first, second], 1).reshape(2 * n, rows, cols)


def sum_low_bits(partial, order, n_pw, me):
    blocks = partial.reshape(n_pw, partial.shape[0] // n_pw, partial.shape[1])
    gone = []
    for number in order:
        place = number - sum(g < number for g in gone)
        kept, sent = halves(blocks, (me >> number) & 1, place)
        got = lax.ppermute(sent.astype(jnp.bfloat16), "pw", flip(n_pw, 1 << number))
        blocks = kept + got.astype(jnp.float32)
        gone.append(number)
    got = lax.ppermute(blocks.astype(jnp.bfloat16), "pw", flip(n_pw, n_pw // 2))
    return (blocks + got.astype(jnp.float32)).astype(jnp.bfloat16)


def exchange(summed, gap_rows, order, n_pair, n_pw, j, me):
    blocks = summed
    left = sorted(order)
    gone = list(order)
    for number in reversed(order):
        gone.remove(number)
        place = number - sum(g < number for g in gone)
        got = lax.ppermute(blocks, "pw", flip(n_pw, 1 << number))
        blocks = merge(blocks, got, (me >> number) & 1, place)
    n, rows, cols = blocks.shape
    own = lax.dynamic_index_in_dim(blocks, me, 0, False)
    tiles = blocks.reshape(n_pair, n * rows // n_pair, cols)
    parts = []
    for d in range(n_pair):
        tile = lax.dynamic_index_in_dim(tiles, j ^ d, 0, False)
        piece = jnp.concatenate([tile, own, gap_rows], 0)
        parts.append(lax.ppermute(piece, "pair", flip(n_pair, d)) if d else piece)
    whole = jnp.concatenate(parts, 1)
    m_rows = tiles.shape[1]
    return whole[m_rows : m_rows + rows], whole[:m_rows], join_gap(whole[m_rows + rows :])


def per_device(
    pair_products, basis, val_energy, cond_energy, frequencies, valence_index, conduction_index
):
    n_pair, n_pw = lax.axis_size("pair"), lax.axis_size("pw")
    j, me = lax.axis_index("pair"), lax.axis_index("pw")
    bits = n_pw.bit_length() - 1
    rows_local = pair_products.shape[1]
    pairs_total = rows_local * n_pair
    block_size = rows_local // GROUPS
    gap = lookup(conduction_index, cond_energy) - lookup(valence_index, val_energy)
    total = None
    for group in range(GROUPS):
        cut = slice(group * block_size, (group + 1) * block_size)
        order = list(range(bits - 1))
        if group % 2:
            order[:2] = order[:2][::-1]
        partial = lax.dot_general(
            basis, pair_products[:, cut], (((0,), (0,)), ((), ())),
            preferred_element_type=jnp.float32,
        )
        summed = sum_low_bits(partial, order, n_pw, me)
        rows_n, rows_m, gaps = exchange(summed, split_gap(gap[cut]), order, n_pair, n_pw, j, me)
        weights = (
            -4.0 * gaps[None, :] / (gaps[None, :] ** 2 + frequencies[:, None] ** 2) / pairs_total
        )
        weighted = (weights[:, None, :] * rows_n.astype(jnp.float32)[None]).astype(jnp.bfloat16)
        part = jnp.einsum("kpc,nc->kpn", weighted, rows_m, preferred_element_type=jnp.float32)
        total = part if total is None else total + part
    return total


def solution(mesh):
    placed = (P("pw", "pair"), P("pw", None), P(), P(), P(), P("pair"), P("pair"))
    return jax.shard_map(
        per_device, mesh=mesh, in_specs=placed, out_specs=P(None, "pw", "pair"), check_vma=False
    )
```

time: 165 us -> 73.8 us (0.45)
  blocking collectives: 92.6 us -> 0 us
  starting transfers between devices: 0.01 us -> 18.8 us
  between operations: 13.5 us -> 0.43 us
  waiting for transfers between devices: 44.5 us -> 37.5 us
    psum x1 -> x0, blocking collectives: 92.6 us -> none  [per_device(): projected_all = lax.psum(partial_sums, 'pw').astype(jnp.bfloat16)]
    reduce_scatter x1 -> x0, waiting for transfers between devices: 44.5 us -> none  [per_device(): lax.psum_scatter(gram_rows, 'pair', scatter_dimension=2, tiled=True)]
    ppermute x0 -> x16, waiting for transfers between devices: none -> 37.5 us  [the longest x6 15.5 us: exchange(): parts.append(lax.ppermute(piece, 'pair', flip(n_pair, d)) if d else piece)]
    ppermute x0 -> x16, starting transfers between devices: none -> 18.8 us  [the longest x2 6.35 us: sum_low_bits(): got = lax.ppermute(blocks.astype(jnp.bfloat16), 'pw', flip(n_pw, n_pw // 2))]
  transfers between devices with their start and end apart: 1 -> 16, of which waited for: 1 -> 13; matrix products, arithmetic and copies ran while one was open for 0% -> 11% of each run, Pallas kernels for 0% -> 0%
where the time goes in v1:
time: 73.8 us; the launch traced here: 73.6 us
  waiting for transfers between devices  37.5 us (51%)
  starting transfers between devices  18.8 us (25%)
  matrix products  15.2 us (21%)
  other arithmetic  1.32 us (2%)
    ppermute x6, waiting for transfers between devices, exchange(): parts.append(lax.ppermute(piece, 'pair', flip(n_pair, d)) if d else piece)  15.5 us
    dot_general x2, matrix products, per_device(): lax.dot_general(basis, pair_products[:, cut], (((0,), (0,)), ((), ())), p...  12.7 us
    ppermute x4, waiting for transfers between devices, exchange(): got = lax.ppermute(blocks, 'pw', flip(n_pw, 1 << number))  8.97 us
    ppermute x4, waiting for transfers between devices, sum_low_bits(): got = lax.ppermute(sent.astype(jnp.bfloat16), 'pw', flip(n_pw, 1 << number))  8.71 us
    ppermute x2, starting transfers between devices, sum_low_bits(): got = lax.ppermute(blocks.astype(jnp.bfloat16), 'pw', flip(n_pw, n_pw // 2))  6.35 us
    ppermute x4, starting transfers between devices, sum_low_bits(): got = lax.ppermute(sent.astype(jnp.bfloat16), 'pw', flip(n_pw, 1 << number))  5.37 us
    ppermute x2, waiting for transfers between devices, sum_low_bits(): got = lax.ppermute(blocks.astype(jnp.bfloat16), 'pw', flip(n_pw, n_pw // 2))  4.32 us
    ppermute x6, starting transfers between devices, exchange(): parts.append(lax.ppermute(piece, 'pair', flip(n_pair, d)) if d else piece)  3.84 us
  transfers between devices with their start and end apart: 16, of which 13 were waited for; matrix products, arithmetic and copies ran while one was open for 11% of the time, Pallas kernels for 0%

profile of v1, /device:TPU:0, one launch (start us, length us, event | category | flops | bytes accessed | tf_op | source)
XLA Modules:
  0.0 73.6 jit_solution(7831241401336606187)
XLA Ops:
  0.0 6.3 %fusion.4 = f32[1024,256]{1,0:T(8,128)S(1)} fusion(bf16[4096,1024]{1,0:T(8,128)(2,1)} %param.8, bf16[4096,512]{1,0:T(8,128)(2,1)} %param.7), kind=kOutput, calls=%fused_computation.6 | convolution fusion | flops 2147483648 | bytes 11534336 | tf_op jit(solution)/shard_map/dot_general | solution.py:102
  6.4 3.1 %collective-permute-start.8 = (bf16[4,128,256]{2,1,0:T(8,128)(2,1)S(1)}, bf16[4,128,256]{2,1,0:T(8,128)(2,1)S(1)}, u32[]{:S(2)}, u32[]{:S(2)}) collective-permute-start(bf16[4,128,256]{2,1,0:T(8,128)(2,1)S(1)} %bitcast.105), channel_id=1, source_target_pairs={{0,2},{1,3},{2,0},{3,1},{4,6},{5,7},{6,4},{7,5},{8,10},{9,11},{10,... | collective-permute-start | bytes 786440 | tf_op jit(solution)/shard_map/ppermute | solution.py:57
  9.5 0.0 copy-start
  9.5 0.0 copy-start.1
  9.5 0.0 copy-start.2
  9.5 0.0 copy-start.3
  9.5 6.4 %fusion.8 = f32[1024,256]{1,0:T(8,128)S(1)} fusion(bf16[4096,1024]{1,0:T(8,128)(2,1)} %param.8, bf16[4096,512]{1,0:T(8,128)(2,1)} %param.7), kind=kOutput, calls=%fused_computation.10 | convolution fusion | flops 2147483648 | bytes 11534336 | tf_op jit(solution)/shard_map/dot_general | solution.py:102
  15.9 1.6 %collective-permute-start = (bf16[4,128,256]{2,1,0:T(8,128)(2,1)S(1)}, bf16[4,128,256]{2,1,0:T(8,128)(2,1)S(1)}, u32[]{:S(2)}, u32[]{:S(2)}) collective-permute-start(bf16[4,128,256]{2,1,0:T(8,128)(2,1)S(1)} %fusion.17), channel_id=1, source_target_pairs={{0,1},{1,0},{2,3},{3,2},{4,5},{5,4},{6,7},{7,6},{8,9},{9,8},{10,11... | collective-permute-start | bytes 786440 | tf_op jit(solution)/shard_map/ppermute | solution.py:57
  17.5 0.0 copy-done
  17.5 0.0 copy-done.1
  17.5 0.0 copy-done.2
  17.5 0.0 copy-done.3
  17.5 0.4 select_reduce_fusion
  18.1 0.0 collective-permute-done.8
  18.2 0.1 bitcast_add_fusion
  18.3 0.6 collective-permute-start.9
  18.8 6.4 %collective-permute-done = bf16[4,128,256]{2,1,0:T(8,128)(2,1)S(1)} collective-permute-done((bf16[4,128,256]{2,1,0:T(8,128)(2,1)S(1)}, bf16[4,128,256]{2,1,0:T(8,128)(2,1)S(1)}, u32[]{:S(2)}, u32[]{:S(2)}) %collective-permute-start) | collective-permute-done | bytes 262176 | tf_op jit(solution)/shard_map/ppermute | solution.py:57
  25.2 0.1 bitcast_add_fusion.1
  25.3 0.1 collective-permute-start.1
  25.4 1.2 %collective-permute-done.9 = bf16[2,128,256]{2,1,0:T(8,128)(2,1)S(1)} collective-permute-done((bf16[2,128,256]{2,1,0:T(8,128)(2,1)S(1)}, bf16[2,128,256]{2,1,0:T(8,128)(2,1)S(1)}, u32[]{:S(2)}, u32[]{:S(2)}) %collective-permute-start.9) | collective-permute-done | bytes 131104 | tf_op jit(solution)/shard_map/ppermute | solution.py:57
  26.6 2.7 %collective-permute-start.10 = (bf16[2,128,256]{2,1,0:T(8,128)(2,1)S(1)}, bf16[2,128,256]{2,1,0:T(8,128)(2,1)S(1)}, u32[]{:S(2)}, u32[]{:S(2)}) collective-permute-start(bf16[2,128,256]{2,1,0:T(8,128)(2,1)S(1)} %fusion.19), channel_id=1, source_target_pairs={{0,4},{1,5},{2,6},{3,7},{4,0},{5,1},{6,2},{7,3},{8,12},{9,13},{10,... | collective-permute-start | bytes 393224 | tf_op jit(solution)/shard_map/ppermute | solution.py:60
  29.3 1.1 %collective-permute-done.1 = bf16[2,128,256]{2,1,0:T(8,128)(2,1)S(1)} collective-permute-done((bf16[2,128,256]{2,1,0:T(8,128)(2,1)S(1)}, bf16[2,128,256]{2,1,0:T(8,128)(2,1)S(1)}, u32[]{:S(2)}, u32[]{:S(2)}) %collective-permute-start.1) | collective-permute-done | bytes 131104 | tf_op jit(solution)/shard_map/ppermute | solution.py:57
  30.4 3.7 %collective-permute-start.2 = (bf16[2,128,256]{2,1,0:T(8,128)(2,1)S(1)}, bf16[2,128,256]{2,1,0:T(8,128)(2,1)S(1)}, u32[]{:S(2)}, u32[]{:S(2)}) collective-permute-start(bf16[2,128,256]{2,1,0:T(8,128)(2,1)S(1)} %fusion.18), channel_id=1, source_target_pairs={{0,4},{1,5},{2,6},{3,7},{4,0},{5,1},{6,2},{7,3},{8,12},{9,13},{10,... | collective-permute-start | bytes 393224 | tf_op jit(solution)/shard_map/ppermute | solution.py:60
  34.1 4.0 %collective-permute-done.10 = bf16[2,128,256]{2,1,0:T(8,128)(2,1)S(1)} collective-permute-done((bf16[2,128,256]{2,1,0:T(8,128)(2,1)S(1)}, bf16[2,128,256]{2,1,0:T(8,128)(2,1)S(1)}, u32[]{:S(2)}, u32[]{:S(2)}) %collective-permute-start.10) | collective-permute-done | bytes 131104 | tf_op jit(solution)/shard_map/ppermute | solution.py:60
  38.2 0.1 add_convert_fusion
  38.2 1.6 %collective-permute-start.11 = (bf16[2,128,256]{2,1,0:T(8,128)(2,1)S(1)}, bf16[2,128,256]{2,1,0:T(8,128)(2,1)S(1)}, u32[]{:S(2)}, u32[]{:S(2)}) collective-permute-start(bf16[2,128,256]{2,1,0:T(8,128)(2,1)S(1)} %add_convert_fusion), channel_id=1, source_target_pairs={{0,1},{1,0},{2,3},{3,2},{4,5},{5,4},{6,7},{7,6},{8,9},{9,8},{10,11... | collective-permute-start | bytes 393224 | tf_op jit(solution)/shard_map/ppermute | solution.py:71
  39.8 0.3 collective-permute-done.2
  40.2 0.1 collective-permute-start.3
  40.2 3.0 %collective-permute-done.11 = bf16[2,128,256]{2,1,0:T(8,128)(2,1)S(1)} collective-permute-done((bf16[2,128,256]{2,1,0:T(8,128)(2,1)S(1)}, bf16[2,128,256]{2,1,0:T(8,128)(2,1)S(1)}, u32[]{:S(2)}, u32[]{:S(2)}) %collective-permute-start.11) | collective-permute-done | bytes 131104 | tf_op jit(solution)/shard_map/ppermute | solution.py:71
  43.3 0.1 collective-permute-start.12
  43.4 3.2 %collective-permute-done.3 = bf16[2,128,256]{2,1,0:T(8,128)(2,1)S(1)} collective-permute-done((bf16[2,128,256]{2,1,0:T(8,128)(2,1)S(1)}, bf16[2,128,256]{2,1,0:T(8,128)(2,1)S(1)}, u32[]{:S(2)}, u32[]{:S(2)}) %collective-permute-start.3) | collective-permute-done | bytes 131104 | tf_op jit(solution)/shard_map/ppermute | solution.py:71
  46.7 1.5 %collective-permute-start.4 = (bf16[4,128,256]{2,1,0:T(8,128)(2,1)S(1)}, bf16[4,128,256]{2,1,0:T(8,128)(2,1)S(1)}, u32[]{:S(2)}, u32[]{:S(2)}) collective-permute-start(bf16[4,128,256]{2,1,0:T(8,128)(2,1)S(1)} %bitcast.97), channel_id=1, source_target_pairs={{0,1},{1,0},{2,3},{3,2},{4,5},{5,4},{6,7},{7,6},{8,9},{9,8},{10,11... | collective-permute-start | bytes 786440 | tf_op jit(solution)/shard_map/ppermute | solution.py:71
  48.1 2.3 %collective-permute-done.12 = bf16[4,128,256]{2,1,0:T(8,128)(2,1)S(1)} collective-permute-done((bf16[4,128,256]{2,1,0:T(8,128)(2,1)S(1)}, bf16[4,128,256]{2,1,0:T(8,128)(2,1)S(1)}, u32[]{:S(2)}, u32[]{:S(2)}) %collective-permute-start.12) | collective-permute-done | bytes 262176 | tf_op jit(solution)/shard_map/ppermute | solution.py:71
  50.5 0.1 broadcast_select_fusion.1
  50.5 0.0 copy-start.4
  50.6 0.1 pad_maximum_fusion.19
  50.7 0.1 collective-permute-start.13
  50.8 1.3 %collective-permute-start.14 = (bf16[400,256]{1,0:T(8,128)(2,1)S(1)}, bf16[400,256]{1,0:T(8,128)(2,1)S(1)}, u32[]{:S(2)}, u32[]{:S(2)}) collective-permute-start(bf16[400,256]{1,0:T(8,128)(2,1)S(1)} %get-tuple-element.29), channel_id=1, source_target_pairs={{0,16},{8,24},{16,0},{24,8},{1,17},{9,25},{17,1},{25,9},{2,18},{10... | collective-permute-start | bytes 614408 | tf_op jit(solution)/shard_map/ppermute | solution.py:80
  52.1 0.5 collective-permute-start.15
  52.7 0.4 collective-permute-done.4
  53.1 0.1 select_bitcast_fusion.1
  53.2 0.1 pad_maximum_fusion.18
  53.4 0.1 pad_maximum_fusion.22
  53.4 0.1 collective-permute-start.5
  53.5 1.4 %collective-permute-start.6 = (bf16[400,256]{1,0:T(8,128)(2,1)S(1)}, bf16[400,256]{1,0:T(8,128)(2,1)S(1)}, u32[]{:S(2)}, u32[]{:S(2)}) collective-permute-start(bf16[400,256]{1,0:T(8,128)(2,1)S(1)} %get-tuple-element.26), channel_id=1, source_target_pairs={{0,16},{8,24},{16,0},{24,8},{1,17},{9,25},{17,1},{25,9},{2,18},{10... | collective-permute-start | bytes 614408 | tf_op jit(solution)/shard_map/ppermute | solution.py:80
  54.9 0.0 collective-permute-done.13
  54.9 0.4 collective-permute-start.7
  55.3 0.0 copy-done.4
  55.4 3.5 %collective-permute-done.14 = bf16[400,256]{1,0:T(8,128)(2,1)S(1)} collective-permute-done((bf16[400,256]{1,0:T(8,128)(2,1)S(1)}, bf16[400,256]{1,0:T(8,128)(2,1)S(1)}, u32[]{:S(2)}, u32[]{:S(2)}) %collective-permute-start.14) | collective-permute-done | bytes 204832 | tf_op jit(solution)/shard_map/ppermute | solution.py:80
  58.8 3.3 %collective-permute-done.15 = bf16[400,256]{1,0:T(8,128)(2,1)S(1)} collective-permute-done((bf16[400,256]{1,0:T(8,128)(2,1)S(1)}, bf16[400,256]{1,0:T(8,128)(2,1)S(1)}, u32[]{:S(2)}, u32[]{:S(2)}) %collective-permute-start.15) | collective-permute-done | bytes 204832 | tf_op jit(solution)/shard_map/ppermute | solution.py:80
  62.2 0.0 collective-permute-done.5
  62.2 5.4 %collective-permute-done.6 = bf16[400,256]{1,0:T(8,128)(2,1)S(1)} collective-permute-done((bf16[400,256]{1,0:T(8,128)(2,1)S(1)}, bf16[400,256]{1,0:T(8,128)(2,1)S(1)}, u32[]{:S(2)}, u32[]{:S(2)}) %collective-permute-start.6) | collective-permute-done | bytes 204832 | tf_op jit(solution)/shard_map/ppermute | solution.py:80
  67.6 3.3 %collective-permute-done.7 = bf16[400,256]{1,0:T(8,128)(2,1)S(1)} collective-permute-done((bf16[400,256]{1,0:T(8,128)(2,1)S(1)}, bf16[400,256]{1,0:T(8,128)(2,1)S(1)}, u32[]{:S(2)}, u32[]{:S(2)}) %collective-permute-start.7) | collective-permute-done | bytes 204832 | tf_op jit(solution)/shard_map/ppermute | solution.py:80
  71.0 0.1 divide_multiply_fusion.1
  71.2 0.7 %fusion.1 = f32[8,128,256]{2,1,0:T(8,128)S(1)} fusion(f32[128,1024]{1,0:T(8,128)S(1)} %maximum_convert_fusion, f32[8,1024]{1,0:T(8,128)S(1)} %get-tuple-element.38, bf16[400,256]{1,0:T(8,128)(2,1)S(1)} %collective-permute-done.15, bf16[400,256]{1,0:T(8,128)(2,1)S(1)} %collective-permute-done.14, bf16[400,256]{1,0:T(8,128)(2,1)S(1)} %collective-permute-done.13, ...), kind=kOutput, calls=%fused_computation.3 | convolution fusion | flops 542113792 | bytes 2424832 | tf_op jit(solution)/shard_map/kpc,nc->kpn/dot_general | solution.py:112
  71.9 1.7 %fusion.10 = f32[8,128,256]{2,1,0:T(8,128)} fusion(f32[8,128,256]{2,1,0:T(8,128)S(1)} %fusion.1, f32[128,1024]{1,0:T(8,128)S(1)} %maximum_convert_fusion.1, f32[8,1024]{1,0:T(8,128)S(1)} %get-tuple-element.37, bf16[400,256]{1,0:T(8,128)(2,1)S(1)} %collective-permute-done.7, bf16[400,256]{1,0:T(8,128)(2,1)S(1)} %collective-permute-done.6, ...), kind=kOutput, calls=%fused_computation.12 | convolution fusion | flops 542375936 | bytes 3473408 | tf_op jit(solution)/shard_map/kpc,nc->kpn/dot_general | solution.py:112
  (37 shorter events, 0.8 us)
Async XLA Ops:
  6.4 11.8 %collective-permute-start.8 = (bf16[4,128,256]{2,1,0:T(8,128)(2,1)S(1)}, bf16[4,128,256]{2,1,0:T(8,128)(2,1)S(1)}, u32[]{:S(2)}, u32[]{:S(2)}) collective-permute-start(bf16[4,128,256]{2,1,0:T(8,128)(2,1)S(1)} %bitcast.105), channel_id=1, source_target_pairs={{0,2},{1,3},{2,0},{3,1},{4,6},{5,7},{6,4},{7,5},{8,10},{9,11},{10,... | collective-permute-start | bytes 786440 | tf_op jit(solution)/shard_map/ppermute | solution.py:57
  9.5 8.0 %copy-start = (s32[512]{0:T(512)S(1)}, s32[512]{0:T(512)}, u32[]{:S(2)}) copy-start(s32[512]{0:T(512)} %param.12) | copy-start | bytes 6148
  9.5 8.0 %copy-start.1 = (s32[512]{0:T(512)S(1)}, s32[512]{0:T(512)}, u32[]{:S(2)}) copy-start(s32[512]{0:T(512)} %param.13) | copy-start | bytes 6148
  9.5 8.0 %copy-start.2 = (f32[128]{0:T(128)S(1)}, f32[128]{0:T(128)}, u32[]{:S(2)}) copy-start(f32[128]{0:T(128)} %param.9) | copy-start | bytes 1540
  9.5 8.0 %copy-start.3 = (f32[128]{0:T(128)S(1)}, f32[128]{0:T(128)}, u32[]{:S(2)}) copy-start(f32[128]{0:T(128)} %param.10) | copy-start | bytes 1540
  15.9 9.2 %collective-permute-start = (bf16[4,128,256]{2,1,0:T(8,128)(2,1)S(1)}, bf16[4,128,256]{2,1,0:T(8,128)(2,1)S(1)}, u32[]{:S(2)}, u32[]{:S(2)}) collective-permute-start(bf16[4,128,256]{2,1,0:T(8,128)(2,1)S(1)} %fusion.17), channel_id=1, source_target_pairs={{0,1},{1,0},{2,3},{3,2},{4,5},{5,4},{6,7},{7,6},{8,9},{9,8},{10,11... | collective-permute-start | bytes 786440 | tf_op jit(solution)/shard_map/ppermute | solution.py:57
  18.3 8.3 %collective-permute-start.9 = (bf16[2,128,256]{2,1,0:T(8,128)(2,1)S(1)}, bf16[2,128,256]{2,1,0:T(8,128)(2,1)S(1)}, u32[]{:S(2)}, u32[]{:S(2)}) collective-permute-start(bf16[2,128,256]{2,1,0:T(8,128)(2,1)S(1)} %fusion.21), channel_id=1, source_target_pairs={{0,1},{1,0},{2,3},{3,2},{4,5},{5,4},{6,7},{7,6},{8,9},{9,8},{10,11... | collective-permute-start | bytes 393224 | tf_op jit(solution)/shard_map/ppermute | solution.py:57
  25.3 5.1 %collective-permute-start.1 = (bf16[2,128,256]{2,1,0:T(8,128)(2,1)S(1)}, bf16[2,128,256]{2,1,0:T(8,128)(2,1)S(1)}, u32[]{:S(2)}, u32[]{:S(2)}) collective-permute-start(bf16[2,128,256]{2,1,0:T(8,128)(2,1)S(1)} %fusion.20), channel_id=1, source_target_pairs={{0,2},{1,3},{2,0},{3,1},{4,6},{5,7},{6,4},{7,5},{8,10},{9,11},{10,... | collective-permute-start | bytes 393224 | tf_op jit(solution)/shard_map/ppermute | solution.py:57
  26.6 11.5 %collective-permute-start.10 = (bf16[2,128,256]{2,1,0:T(8,128)(2,1)S(1)}, bf16[2,128,256]{2,1,0:T(8,128)(2,1)S(1)}, u32[]{:S(2)}, u32[]{:S(2)}) collective-permute-start(bf16[2,128,256]{2,1,0:T(8,128)(2,1)S(1)} %fusion.19), channel_id=1, source_target_pairs={{0,4},{1,5},{2,6},{3,7},{4,0},{5,1},{6,2},{7,3},{8,12},{9,13},{10,... | collective-permute-start | bytes 393224 | tf_op jit(solution)/shard_map/ppermute | solution.py:60
  30.4 9.7 %collective-permute-start.2 = (bf16[2,128,256]{2,1,0:T(8,128)(2,1)S(1)}, bf16[2,128,256]{2,1,0:T(8,128)(2,1)S(1)}, u32[]{:S(2)}, u32[]{:S(2)}) collective-permute-start(bf16[2,128,256]{2,1,0:T(8,128)(2,1)S(1)} %fusion.18), channel_id=1, source_target_pairs={{0,4},{1,5},{2,6},{3,7},{4,0},{5,1},{6,2},{7,3},{8,12},{9,13},{10,... | collective-permute-start | bytes 393224 | tf_op jit(solution)/shard_map/ppermute | solution.py:60
  38.2 5.0 %collective-permute-start.11 = (bf16[2,128,256]{2,1,0:T(8,128)(2,1)S(1)}, bf16[2,128,256]{2,1,0:T(8,128)(2,1)S(1)}, u32[]{:S(2)}, u32[]{:S(2)}) collective-permute-start(bf16[2,128,256]{2,1,0:T(8,128)(2,1)S(1)} %add_convert_fusion), channel_id=1, source_target_pairs={{0,1},{1,0},{2,3},{3,2},{4,5},{5,4},{6,7},{7,6},{8,9},{9,8},{10,11... | collective-permute-start | bytes 393224 | tf_op jit(solution)/shard_map/ppermute | solution.py:71
  40.2 6.4 %collective-permute-start.3 = (bf16[2,128,256]{2,1,0:T(8,128)(2,1)S(1)}, bf16[2,128,256]{2,1,0:T(8,128)(2,1)S(1)}, u32[]{:S(2)}, u32[]{:S(2)}) collective-permute-start(bf16[2,128,256]{2,1,0:T(8,128)(2,1)S(1)} %add_convert_fusion.1), channel_id=1, source_target_pairs={{0,2},{1,3},{2,0},{3,1},{4,6},{5,7},{6,4},{7,5},{8,10},{9,11},{10,... | collective-permute-start | bytes 393224 | tf_op jit(solution)/shard_map/ppermute | solution.py:71
  43.3 7.1 %collective-permute-start.12 = (bf16[4,128,256]{2,1,0:T(8,128)(2,1)S(1)}, bf16[4,128,256]{2,1,0:T(8,128)(2,1)S(1)}, u32[]{:S(2)}, u32[]{:S(2)}) collective-permute-start(bf16[4,128,256]{2,1,0:T(8,128)(2,1)S(1)} %bitcast.98), channel_id=1, source_target_pairs={{0,2},{1,3},{2,0},{3,1},{4,6},{5,7},{6,4},{7,5},{8,10},{9,11},{10,... | collective-permute-start | bytes 786440 | tf_op jit(solution)/shard_map/ppermute | solution.py:71
  46.7 6.4 %collective-permute-start.4 = (bf16[4,128,256]{2,1,0:T(8,128)(2,1)S(1)}, bf16[4,128,256]{2,1,0:T(8,128)(2,1)S(1)}, u32[]{:S(2)}, u32[]{:S(2)}) collective-permute-start(bf16[4,128,256]{2,1,0:T(8,128)(2,1)S(1)} %bitcast.97), channel_id=1, source_target_pairs={{0,1},{1,0},{2,3},{3,2},{4,5},{5,4},{6,7},{7,6},{8,9},{9,8},{10,11... | collective-permute-start | bytes 786440 | tf_op jit(solution)/shard_map/ppermute | solution.py:71
  50.5 4.8 %copy-start.4 = (f32[8]{0:T(128)S(1)}, f32[8]{0:T(128)}, u32[]{:S(2)}) copy-start(f32[8]{0:T(128)} %param.11) | copy-start | bytes 100
  50.7 4.2 %collective-permute-start.13 = (bf16[400,256]{1,0:T(8,128)(2,1)S(1)}, bf16[400,256]{1,0:T(8,128)(2,1)S(1)}, u32[]{:S(2)}, u32[]{:S(2)}) collective-permute-start(bf16[400,256]{1,0:T(8,128)(2,1)S(1)} %get-tuple-element.28), channel_id=1, source_target_pairs={{0,8},{8,0},{16,24},{24,16},{1,9},{9,1},{17,25},{25,17},{2,10},{10... | collective-permute-start | bytes 614408 | tf_op jit(solution)/shard_map/ppermute | solution.py:80
  50.8 8.0 %collective-permute-start.14 = (bf16[400,256]{1,0:T(8,128)(2,1)S(1)}, bf16[400,256]{1,0:T(8,128)(2,1)S(1)}, u32[]{:S(2)}, u32[]{:S(2)}) collective-permute-start(bf16[400,256]{1,0:T(8,128)(2,1)S(1)} %get-tuple-element.29), channel_id=1, source_target_pairs={{0,16},{8,24},{16,0},{24,8},{1,17},{9,25},{17,1},{25,9},{2,18},{10... | collective-permute-start | bytes 614408 | tf_op jit(solution)/shard_map/ppermute | solution.py:80
  52.1 10.0 %collective-permute-start.15 = (bf16[400,256]{1,0:T(8,128)(2,1)S(1)}, bf16[400,256]{1,0:T(8,128)(2,1)S(1)}, u32[]{:S(2)}, u32[]{:S(2)}) collective-permute-start(bf16[400,256]{1,0:T(8,128)(2,1)S(1)} %get-tuple-element.30), channel_id=1, source_target_pairs={{0,24},{8,16},{16,8},{24,0},{1,25},{9,17},{17,9},{25,1},{2,26},{10... | collective-permute-start | bytes 614408 | tf_op jit(solution)/shard_map/ppermute | solution.py:80
  53.4 8.8 %collective-permute-start.5 = (bf16[400,256]{1,0:T(8,128)(2,1)S(1)}, bf16[400,256]{1,0:T(8,128)(2,1)S(1)}, u32[]{:S(2)}, u32[]{:S(2)}) collective-permute-start(bf16[400,256]{1,0:T(8,128)(2,1)S(1)} %get-tuple-element.25), channel_id=1, source_target_pairs={{0,8},{8,0},{16,24},{24,16},{1,9},{9,1},{17,25},{25,17},{2,10},{10... | collective-permute-start | bytes 614408 | tf_op jit(solution)/shard_map/ppermute | solution.py:80
  53.5 14.1 %collective-permute-start.6 = (bf16[400,256]{1,0:T(8,128)(2,1)S(1)}, bf16[400,256]{1,0:T(8,128)(2,1)S(1)}, u32[]{:S(2)}, u32[]{:S(2)}) collective-permute-start(bf16[400,256]{1,0:T(8,128)(2,1)S(1)} %get-tuple-element.26), channel_id=1, source_target_pairs={{0,16},{8,24},{16,0},{24,8},{1,17},{9,25},{17,1},{25,9},{2,18},{10... | collective-permute-start | bytes 614408 | tf_op jit(solution)/shard_map/ppermute | solution.py:80
  54.9 16.0 %collective-permute-start.7 = (bf16[400,256]{1,0:T(8,128)(2,1)S(1)}, bf16[400,256]{1,0:T(8,128)(2,1)S(1)}, u32[]{:S(2)}, u32[]{:S(2)}) collective-permute-start(bf16[400,256]{1,0:T(8,128)(2,1)S(1)} %get-tuple-element.27), channel_id=1, source_target_pairs={{0,24},{8,16},{16,8},{24,0},{1,25},{9,17},{17,9},{25,1},{2,26},{10... | collective-permute-start | bytes 614408 | tf_op jit(solution)/shard_map/ppermute | solution.py:80

commit v2 on v1

--- a/solution.py
+++ b/solution.py
@@ -1,9 +1,12 @@
 import jax
 import jax.numpy as jnp
 from jax import lax
+from jax.experimental import pallas as pl
+from jax.experimental.pallas import tpu as pltpu
 from jax.sharding import PartitionSpec as P
 
 GROUPS = 2
+LOADS = 8
 GAP_ROWS = 16
 
 
@@ -48,12 +51,79 @@
     return jnp.concatenate([first, second], 1).reshape(2 * n, rows, cols)
 
 
-def sum_low_bits(partial, order, n_pw, me):
-    blocks = partial.reshape(n_pw, partial.shape[0] // n_pw, partial.shape[1])
+def with_bit(index, bit, place):
+    return ((index >> place) << (place + 1)) | (bit << place) | (index & ((1 << place) - 1))
+
+
+def project_body(me_ref, basis_ref, pairs_ref, *refs, firsts, n_pw):
+    outs = refs[: 2 * len(firsts)]
+    basis_mem, pairs_mem, acc, sems = refs[2 * len(firsts) :]
+    step = basis_mem.shape[0] // LOADS
+    spans = [pl.ds(n * step, step) for n in range(LOADS)]
+    copies = [
+        [
+            pltpu.make_async_copy(basis_ref.at[span], basis_mem.at[span], sems.at[0, n]),
+            pltpu.make_async_copy(pairs_ref.at[span], pairs_mem.at[span], sems.at[1, n]),
+        ]
+        for n, span in enumerate(spans)
+    ]
+    for both in copies:
+        for copy in both:
+            copy.start()
+    for n, span in enumerate(spans):
+        for copy in copies[n]:
+            copy.wait()
+        product = lax.dot_general(
+            basis_mem[span], pairs_mem[span], (((0,), (0,)), ((), ())),
+            preferred_element_type=jnp.float32,
+        )
+        acc[...] = product if n == 0 else acc[...] + product
+    rows = acc.shape[0] // n_pw
+    cols = acc.shape[1] // len(firsts)
+    for group, first in enumerate(firsts):
+        kept_ref, sent_ref = outs[2 * group], outs[2 * group + 1]
+        span = pl.ds(group * cols, cols)
+        bit = (me_ref[0] >> first) & 1
+        for q in range(n_pw // 2):
+            mine = pl.multiple_of(with_bit(q, bit, first) * rows, rows)
+            other = pl.multiple_of(with_bit(q, 1 - bit, first) * rows, rows)
+            kept_ref[q] = acc[pl.ds(mine, rows), span]
+            sent_ref[q] = acc[pl.ds(other, rows), span].astype(jnp.bfloat16)
+
+
+def project(basis, pair_products, me, firsts, n_pw):
+    depth, rows_all = basis.shape
+    cols_all = pair_products.shape[1]
+    shape = (n_pw // 2, rows_all // n_pw, cols_all // len(firsts))
+    outs = []
+    for _ in firsts:
+        outs += [jax.ShapeDtypeStruct(shape, jnp.float32), jax.ShapeDtypeStruct(shape, jnp.bfloat16)]
+    body = lambda *refs: project_body(*refs, firsts=firsts, n_pw=n_pw)
+    flat = pl.pallas_call(
+        body,
+        in_specs=[
+            pl.BlockSpec(memory_space=pltpu.SMEM),
+            pl.BlockSpec(memory_space=pl.ANY),
+            pl.BlockSpec(memory_space=pl.ANY),
+        ],
+        out_shape=outs,
+        scratch_shapes=[
+            pltpu.VMEM(basis.shape, basis.dtype),
+            pltpu.VMEM(pair_products.shape, pair_products.dtype),
+            pltpu.VMEM((rows_all, cols_all), jnp.float32),
+            pltpu.SemaphoreType.DMA((2, LOADS)),
+        ],
+        name="project",
+    )(me.astype(jnp.int32)[None], basis, pair_products)
+    return [(flat[2 * g], flat[2 * g + 1]) for g in range(len(firsts))]
+
+
+def sum_low_bits(kept, sent, order, n_pw, me):
     gone = []
     for number in order:
         place = number - sum(g < number for g in gone)
-        kept, sent = halves(blocks, (me >> number) & 1, place)
+        if gone:
+            kept, sent = halves(blocks, (me >> number) & 1, place)
         got = lax.ppermute(sent.astype(jnp.bfloat16), "pw", flip(n_pw, 1 << number))
         blocks = kept + got.astype(jnp.float32)
         gone.append(number)
@@ -83,6 +153,39 @@
     return whole[m_rows : m_rows + rows], whole[:m_rows], join_gap(whole[m_rows + rows :])
 
 
+def exchange_square(summed, gap_rows, n_pair, n_pw, j, me):
+    chip, core = j >> 1, j & 1
+    far, near, side = me >> 2, (me >> 1) & 1, me & 1
+    n, rows, cols = summed.shape
+    own = jnp.concatenate([summed.reshape(n * rows, cols), gap_rows], 0)
+    across = lax.ppermute(own, "pair", flip(n_pair, 2))
+    both = jnp.concatenate([own, across], 1)
+    twin = lax.ppermute(both, "pair", flip(n_pair, 1))
+    whole = jnp.concatenate(
+        [jnp.where(core == 0, both, twin), jnp.where(core == 0, twin, both)], 1
+    )
+    blocks = whole[: n * rows].reshape(n, rows, 2 * both.shape[1])
+    rows_n = lax.dynamic_index_in_dim(blocks, far, 0, False)
+    mine = lax.dynamic_index_in_dim(blocks, chip, 0, False)
+    hop, diagonal = [], []
+    for a in range(n_pair):
+        for b in range(n_pw):
+            if (a & 1) == (b >> 1) & 1:
+                hop.append((a * n_pw + b, a * n_pw + (b ^ 1)))
+                diagonal.append((a * n_pw + b, a * n_pw + (b ^ 3)))
+            else:
+                hop.append((a * n_pw + b, (a ^ 1) * n_pw + (b ^ 2)))
+    first = lax.ppermute(mine, ("pair", "pw"), hop)
+    second = lax.ppermute(mine, ("pair", "pw"), diagonal)
+    here = core == near
+    same = jnp.where(here, mine, first)
+    other = jnp.where(here, first, second)
+    rows_m = jnp.concatenate(
+        [jnp.where(side == 0, same, other), jnp.where(side == 0, other, same)], 0
+    )
+    return rows_n, rows_m, join_gap(whole[n * rows :])
+
+
 def per_device(
     pair_products, basis, val_energy, cond_energy, frequencies, valence_index, conduction_index
 ):
@@ -94,17 +197,21 @@
     block_size = rows_local // GROUPS
     gap = lookup(conduction_index, cond_energy) - lookup(valence_index, val_energy)
     total = None
+    orders = []
     for group in range(GROUPS):
-        cut = slice(group * block_size, (group + 1) * block_size)
         order = list(range(bits - 1))
         if group % 2:
             order[:2] = order[:2][::-1]
-        partial = lax.dot_general(
-            basis, pair_products[:, cut], (((0,), (0,)), ((), ())),
-            preferred_element_type=jnp.float32,
-        )
-        summed = sum_low_bits(partial, order, n_pw, me)
-        rows_n, rows_m, gaps = exchange(summed, split_gap(gap[cut]), order, n_pair, n_pw, j, me)
+        orders.append(order)
+    partials = project(basis, pair_products, me, [order[0] for order in orders], n_pw)
+    for group, order in enumerate(orders):
+        cut = slice(group * block_size, (group + 1) * block_size)
+        summed = sum_low_bits(*partials[group], order, n_pw, me)
+        gap_rows = split_gap(gap[cut])
+        if n_pair.bit_length() == 3 and n_pw.bit_length() == 4:
+            rows_n, rows_m, gaps = exchange_square(summed, gap_rows, n_pair, n_pw, j, me)
+        else:
+            rows_n, rows_m, gaps = exchange(summed, gap_rows, order, n_pair, n_pw, j, me)
         weights = (
             -4.0 * gaps[None, :] / (gaps[None, :] ** 2 + frequencies[:, None] ** 2) / pairs_total
         )

time: 73.8 us -> 66.7 us (0.904)
  matrix products: 15.2 us -> 2.48 us
  waiting for transfers between devices: 37.5 us -> 28.4 us
  Pallas kernels: 0 us -> 7.93 us
  starting transfers between devices: 18.8 us -> 23.7 us
  other arithmetic: 1.32 us -> 3.52 us
    dot_general x2 -> x0, matrix products: 12.7 us -> none  [per_device(): lax.dot_general(basis, pair_products[:, cut], (((0,), (0,)), ((), ())), p...]
    pallas_call x0 -> x1, Pallas kernels: none -> 7.93 us  [project(): pl.pallas_call(body, in_specs=[pl.BlockSpec(memory_space=pltpu.SMEM), pl....]
    ppermute x10 -> x8, waiting for transfers between devices: 24.5 us -> 17.6 us  [the longest x2 8.2 us: exchange_square(): across = lax.ppermute(own, 'pair', flip(n_pair, 2))]
    ppermute x4, waiting for transfers between devices: 8.71 us -> 4.96 us  [sum_low_bits(): got = lax.ppermute(sent.astype(jnp.bfloat16), 'pw', flip(n_pw, 1 << number))]
    ppermute x10 -> x8, starting transfers between devices: 7.03 us -> 10.1 us  [the longest x2 5.71 us: exchange_square(): second = lax.ppermute(mine, ('pair', 'pw'), diagonal)]
    ppermute x4, starting transfers between devices: 5.37 us -> 8.08 us  [sum_low_bits(): got = lax.ppermute(sent.astype(jnp.bfloat16), 'pw', flip(n_pw, 1 << number))]
    add x2, other arithmetic: 0.12 us -> 2.19 us  [sum_low_bits(): blocks = kept + got.astype(jnp.float32)]
    ppermute x2, waiting for transfers between devices: 4.32 us -> 5.84 us  [sum_low_bits(): got = lax.ppermute(blocks.astype(jnp.bfloat16), 'pw', flip(n_pw, n_pw // 2))]
  transfers between devices with their start and end apart: 16 -> 14, of which waited for: 13 -> 10; matrix products, arithmetic and copies ran while one was open for 11% -> 6% of each run, Pallas kernels for 0% -> 0%
where the time goes in v2:
time: 66.7 us; the launch traced here: 66.4 us
  waiting for transfers between devices  28.4 us (43%)
  starting transfers between devices  23.7 us (36%)
  Pallas kernels  7.93 us (12%)
  other arithmetic  3.52 us (5%)
  matrix products  2.48 us (4%)
    ppermute x2, waiting for transfers between devices, exchange_square(): across = lax.ppermute(own, 'pair', flip(n_pair, 2))  8.2 us
    ppermute x4, starting transfers between devices, sum_low_bits(): got = lax.ppermute(sent.astype(jnp.bfloat16), 'pw', flip(n_pw, 1 << number))  8.08 us
    pallas_call x1, Pallas kernels, project(): pl.pallas_call(body, in_specs=[pl.BlockSpec(memory_space=pltpu.SMEM), pl....  7.93 us
    ppermute x2, waiting for transfers between devices, exchange_square(): first = lax.ppermute(mine, ('pair', 'pw'), hop)  6.63 us
    ppermute x2, waiting for transfers between devices, sum_low_bits(): got = lax.ppermute(blocks.astype(jnp.bfloat16), 'pw', flip(n_pw, n_pw // 2))  5.84 us
    ppermute x2, starting transfers between devices, exchange_square(): second = lax.ppermute(mine, ('pair', 'pw'), diagonal)  5.71 us
    ppermute x2, starting transfers between devices, sum_low_bits(): got = lax.ppermute(blocks.astype(jnp.bfloat16), 'pw', flip(n_pw, n_pw // 2))  5.53 us
    ppermute x4, waiting for transfers between devices, sum_low_bits(): got = lax.ppermute(sent.astype(jnp.bfloat16), 'pw', flip(n_pw, 1 << number))  4.96 us
  transfers between devices with their start and end apart: 14, of which 10 were waited for; matrix products, arithmetic and copies ran while one was open for 6% of the time, Pallas kernels for 0%

profile of v2, /device:TPU:0, one launch (start us, length us, event | category | flops | bytes accessed | tf_op | source)
XLA Modules:
  0.0 66.4 jit_solution(1953212334353663737)
XLA Ops:
  0.0 0.0 copy-start
  0.0 0.0 copy-start.1
  0.0 0.0 copy-start.2
  0.0 0.0 copy-start.3
  0.0 7.9 %project.1 = (f32[4,128,256]{2,1,0:T(8,128)}, bf16[4,128,256]{2,1,0:T(8,128)(2,1)}, f32[4,128,256]{2,1,0:T(8,128)}, bf16[4,128,256]{2,1,0:T(8,128)(2,1)}) custom-call(s32[1]{0:T(128)} %bitcast.refs_0_, bf16[4096,1024]{1,0:T(8,128)(2,1)} %refs_1_.1, bf16[4096,512]{1,0:T(8,128)(2,1)} %refs_2_.1), custom_call_target="tpu_custom_call" | custom-call | tf_op jit(solution)/shard_map/project/pallas_call | solution.py:102
  7.9 0.0 copy-start.4
  8.0 3.1 %collective-permute-start = (bf16[4,128,256]{2,1,0:T(8,128)(2,1)}, bf16[4,128,256]{2,1,0:T(8,128)(2,1)S(1)}, u32[]{:S(2)}, u32[]{:S(2)}) collective-permute-start(bf16[4,128,256]{2,1,0:T(8,128)(2,1)} %get-tuple-element.10), channel_id=1, source_target_pairs={{0,1},{1,0},{2,3},{3,2},{4,5},{5,4},{6,7},{7,6},{8,9},{9,8},{10,11... | collective-permute-start | bytes 786440 | tf_op jit(solution)/shard_map/ppermute | solution.py:127
  11.0 1.6 %collective-permute-start.7 = (bf16[4,128,256]{2,1,0:T(8,128)(2,1)}, bf16[4,128,256]{2,1,0:T(8,128)(2,1)S(1)}, u32[]{:S(2)}, u32[]{:S(2)}) collective-permute-start(bf16[4,128,256]{2,1,0:T(8,128)(2,1)} %get-tuple-element.12), channel_id=1, source_target_pairs={{0,2},{1,3},{2,0},{3,1},{4,6},{5,7},{6,4},{7,5},{8,10},{9,11},{10,... | collective-permute-start | bytes 786440 | tf_op jit(solution)/shard_map/ppermute | solution.py:127
  12.6 0.0 copy-done
  12.6 0.0 copy-done.1
  12.6 0.0 copy-done.2
  12.6 0.0 copy-done.3
  12.6 0.4 select_reduce_fusion
  13.1 4.4 %collective-permute-done = bf16[4,128,256]{2,1,0:T(8,128)(2,1)S(1)} collective-permute-done((bf16[4,128,256]{2,1,0:T(8,128)(2,1)}, bf16[4,128,256]{2,1,0:T(8,128)(2,1)S(1)}, u32[]{:S(2)}, u32[]{:S(2)}) %collective-permute-start) | collective-permute-done | bytes 262176 | tf_op jit(solution)/shard_map/ppermute | solution.py:127
  17.5 1.1 %convert_add_fusion.1 = f32[4,128,256]{2,1,0:T(8,128)S(1)} fusion(f32[4,128,256]{2,1,0:T(8,128)} %get-tuple-element.9, bf16[4,128,256]{2,1,0:T(8,128)(2,1)S(1)} %collective-permute-done), kind=kLoop, calls=%fused_computation.18 | loop fusion | flops 262144 | bytes 1310720 | tf_op jit(solution)/shard_map/add | solution.py:128
  18.7 1.9 %collective-permute-start.1 = (bf16[2,128,256]{2,1,0:T(8,128)(2,1)S(1)}, bf16[2,128,256]{2,1,0:T(8,128)(2,1)S(1)}, u32[]{:S(2)}, u32[]{:S(2)}) collective-permute-start(bf16[2,128,256]{2,1,0:T(8,128)(2,1)S(1)} %fusion.13), channel_id=1, source_target_pairs={{0,2},{1,3},{2,0},{3,1},{4,6},{5,7},{6,4},{7,5},{8,10},{9,11},{10,... | collective-permute-start | bytes 393224 | tf_op jit(solution)/shard_map/ppermute | solution.py:127
  20.5 0.0 collective-permute-done.7
  20.5 1.1 %convert_add_fusion = f32[4,128,256]{2,1,0:T(8,128)S(1)} fusion(f32[4,128,256]{2,1,0:T(8,128)} %get-tuple-element.11, bf16[4,128,256]{2,1,0:T(8,128)(2,1)S(1)} %collective-permute-done.7), kind=kLoop, calls=%fused_computation.17 | loop fusion | flops 262144 | bytes 1310720 | tf_op jit(solution)/shard_map/add | solution.py:128
  21.7 1.6 %collective-permute-start.8 = (bf16[2,128,256]{2,1,0:T(8,128)(2,1)S(1)}, bf16[2,128,256]{2,1,0:T(8,128)(2,1)S(1)}, u32[]{:S(2)}, u32[]{:S(2)}) collective-permute-start(bf16[2,128,256]{2,1,0:T(8,128)(2,1)S(1)} %fusion.14), channel_id=1, source_target_pairs={{0,1},{1,0},{2,3},{3,2},{4,5},{5,4},{6,7},{7,6},{8,9},{9,8},{10,11... | collective-permute-start | bytes 393224 | tf_op jit(solution)/shard_map/ppermute | solution.py:127
  23.2 0.5 collective-permute-done.1
  23.7 2.9 %collective-permute-start.2 = (bf16[2,128,256]{2,1,0:T(8,128)(2,1)S(1)}, bf16[2,128,256]{2,1,0:T(8,128)(2,1)S(1)}, u32[]{:S(2)}, u32[]{:S(2)}) collective-permute-start(bf16[2,128,256]{2,1,0:T(8,128)(2,1)S(1)} %fusion.11), channel_id=1, source_target_pairs={{0,4},{1,5},{2,6},{3,7},{4,0},{5,1},{6,2},{7,3},{8,12},{9,13},{10,... | collective-permute-start | bytes 393224 | tf_op jit(solution)/shard_map/ppermute | solution.py:130
  26.6 0.1 collective-permute-done.8
  26.7 2.7 %collective-permute-start.9 = (bf16[2,128,256]{2,1,0:T(8,128)(2,1)S(1)}, bf16[2,128,256]{2,1,0:T(8,128)(2,1)S(1)}, u32[]{:S(2)}, u32[]{:S(2)}) collective-permute-start(bf16[2,128,256]{2,1,0:T(8,128)(2,1)S(1)} %fusion.12), channel_id=1, source_target_pairs={{0,4},{1,5},{2,6},{3,7},{4,0},{5,1},{6,2},{7,3},{8,12},{9,13},{10,... | collective-permute-start | bytes 393224 | tf_op jit(solution)/shard_map/ppermute | solution.py:130
  29.4 5.8 %collective-permute-done.2 = bf16[2,128,256]{2,1,0:T(8,128)(2,1)S(1)} collective-permute-done((bf16[2,128,256]{2,1,0:T(8,128)(2,1)S(1)}, bf16[2,128,256]{2,1,0:T(8,128)(2,1)S(1)}, u32[]{:S(2)}, u32[]{:S(2)}) %collective-permute-start.2) | collective-permute-done | bytes 131104 | tf_op jit(solution)/shard_map/ppermute | solution.py:130
  35.3 1.5 %collective-permute-start.3 = (bf16[272,256]{1,0:T(8,128)(2,1)S(1)}, bf16[272,256]{1,0:T(8,128)(2,1)S(1)}, u32[]{:S(2)}, u32[]{:S(2)}) collective-permute-start(bf16[272,256]{1,0:T(8,128)(2,1)S(1)} %pad_maximum_fusion.4), channel_id=1, source_target_pairs={{0,16},{8,24},{16,0},{24,8},{1,17},{9,25},{17,1},{25,9},{2,18},{10... | collective-permute-start | bytes 417800 | tf_op jit(solution)/shard_map/ppermute | solution.py:161
  36.8 0.0 collective-permute-done.9
  36.8 0.1 add_convert_fusion
  36.8 3.6 %collective-permute-done.3 = bf16[272,256]{1,0:T(8,128)(2,1)S(1)} collective-permute-done((bf16[272,256]{1,0:T(8,128)(2,1)S(1)}, bf16[272,256]{1,0:T(8,128)(2,1)S(1)}, u32[]{:S(2)}, u32[]{:S(2)}) %collective-permute-start.3) | collective-permute-done | bytes 139296 | tf_op jit(solution)/shard_map/ppermute | solution.py:161
  40.4 0.1 collective-permute-start.4
  40.5 1.5 %collective-permute-start.10 = (bf16[272,256]{1,0:T(8,128)(2,1)S(1)}, bf16[272,256]{1,0:T(8,128)(2,1)S(1)}, u32[]{:S(2)}, u32[]{:S(2)}) collective-permute-start(bf16[272,256]{1,0:T(8,128)(2,1)S(1)} %pad_maximum_fusion.5), channel_id=1, source_target_pairs={{0,16},{8,24},{16,0},{24,8},{1,17},{9,25},{17,1},{25,9},{2,18},{10... | collective-permute-start | bytes 417800 | tf_op jit(solution)/shard_map/ppermute | solution.py:161
  42.0 0.0 copy-done.4
  42.0 4.6 %collective-permute-done.10 = bf16[272,256]{1,0:T(8,128)(2,1)S(1)} collective-permute-done((bf16[272,256]{1,0:T(8,128)(2,1)S(1)}, bf16[272,256]{1,0:T(8,128)(2,1)S(1)}, u32[]{:S(2)}, u32[]{:S(2)}) %collective-permute-start.10) | collective-permute-done | bytes 139296 | tf_op jit(solution)/shard_map/ppermute | solution.py:161
  46.7 0.1 collective-permute-start.11
  46.8 0.0 collective-permute-done.4
  46.8 0.1 broadcast_select_fusion.3
  46.9 0.1 pad_maximum_fusion.1
  47.0 0.1 dynamic-slice_bitcast_fusion.1
  47.0 3.3 %collective-permute-start.6 = (bf16[128,1024]{1,0:T(8,128)(2,1)S(1)}, bf16[128,1024]{1,0:T(8,128)(2,1)S(1)}, u32[]{:S(2)}, u32[]{:S(2)}) collective-permute-start(bf16[128,1024]{1,0:T(8,128)(2,1)S(1)} %get-tuple-element.27), channel_id=1, source_target_pairs={{0,3},{1,2},{4,7},{5,6},{10,9},{11,8},{14,13},{15,12},{16,19},{17,... | collective-permute-start | bytes 786440 | tf_op jit(solution)/shard_map/ppermute | solution.py:179
  50.3 0.6 collective-permute-start.5
  50.9 0.0 collective-permute-done.11
  50.9 0.1 broadcast_select_fusion.1
  51.0 0.1 pad_maximum_fusion
  51.1 0.1 dynamic-slice_bitcast_fusion
  51.2 2.4 %collective-permute-start.13 = (bf16[128,1024]{1,0:T(8,128)(2,1)S(1)}, bf16[128,1024]{1,0:T(8,128)(2,1)S(1)}, u32[]{:S(2)}, u32[]{:S(2)}) collective-permute-start(bf16[128,1024]{1,0:T(8,128)(2,1)S(1)} %get-tuple-element.25), channel_id=1, source_target_pairs={{0,3},{1,2},{4,7},{5,6},{10,9},{11,8},{14,13},{15,12},{16,19},{17,... | collective-permute-start | bytes 786440 | tf_op jit(solution)/shard_map/ppermute | solution.py:179
  53.6 0.6 collective-permute-start.12
  54.3 0.1 divide_multiply_fusion
  54.4 2.6 %collective-permute-done.6 = bf16[128,1024]{1,0:T(8,128)(2,1)S(1)} collective-permute-done((bf16[128,1024]{1,0:T(8,128)(2,1)S(1)}, bf16[128,1024]{1,0:T(8,128)(2,1)S(1)}, u32[]{:S(2)}, u32[]{:S(2)}) %collective-permute-start.6) | collective-permute-done | bytes 262176 | tf_op jit(solution)/shard_map/ppermute | solution.py:179
  57.0 2.6 %collective-permute-done.5 = bf16[128,1024]{1,0:T(8,128)(2,1)S(1)} collective-permute-done((bf16[128,1024]{1,0:T(8,128)(2,1)S(1)}, bf16[128,1024]{1,0:T(8,128)(2,1)S(1)}, u32[]{:S(2)}, u32[]{:S(2)}) %collective-permute-start.5) | collective-permute-done | bytes 262176 | tf_op jit(solution)/shard_map/ppermute | solution.py:178
  59.5 0.1 broadcast_select_fusion.11
  59.6 0.8 %fusion = f32[8,128,256]{2,1,0:T(8,128)S(1)} fusion(f32[128,1024]{1,0:T(8,128)S(1)} %get-tuple-element.28, f32[8,1024]{1,0:T(8,128)S(1)} %get-tuple-element.36, bf16[128,1024]{1,0:T(8,128)(2,1)S(1)} %get-tuple-element.20, bf16[128,1024]{1,0:T(8,128)(2,1)S(1)} %get-tuple-element.19), kind=kOutput, calls=%fused_computation.2 | convolution fusion | flops 540016640 | bytes 2129920 | tf_op jit(solution)/shard_map/kpc,nc->kpn/dot_general | solution.py:219
  60.4 0.2 collective-permute-done.13
  60.6 4.1 %collective-permute-done.12 = bf16[128,1024]{1,0:T(8,128)(2,1)S(1)} collective-permute-done((bf16[128,1024]{1,0:T(8,128)(2,1)S(1)}, bf16[128,1024]{1,0:T(8,128)(2,1)S(1)}, u32[]{:S(2)}, u32[]{:S(2)}) %collective-permute-start.12) | collective-permute-done | bytes 262176 | tf_op jit(solution)/shard_map/ppermute | solution.py:178
  64.6 0.1 broadcast_select_fusion.9
  64.7 1.7 %fusion.6 = f32[8,128,256]{2,1,0:T(8,128)} fusion(f32[8,128,256]{2,1,0:T(8,128)S(1)} %fusion, f32[128,1024]{1,0:T(8,128)S(1)} %get-tuple-element.26, f32[8,1024]{1,0:T(8,128)S(1)} %get-tuple-element.35, bf16[128,1024]{1,0:T(8,128)(2,1)S(1)} %get-tuple-element.18, bf16[128,1024]{1,0:T(8,128)(2,1)S(1)} %get-tuple-element.17), kind=kOutput, calls=%fused_computation.8 | convolution fusion | flops 540278784 | bytes 3178496 | tf_op jit(solution)/shard_map/kpc,nc->kpn/dot_general | solution.py:219
  (24 shorter events, 0.3 us)
Async XLA Ops:
  0.0 12.6 %copy-start = (s32[512]{0:T(512)S(1)}, s32[512]{0:T(512)}, u32[]{:S(2)}) copy-start(s32[512]{0:T(512)} %param.12) | copy-start | bytes 6148
  0.0 12.6 %copy-start.1 = (s32[512]{0:T(512)S(1)}, s32[512]{0:T(512)}, u32[]{:S(2)}) copy-start(s32[512]{0:T(512)} %param.13) | copy-start | bytes 6148
  0.0 12.6 %copy-start.2 = (f32[128]{0:T(128)S(1)}, f32[128]{0:T(128)}, u32[]{:S(2)}) copy-start(f32[128]{0:T(128)} %param.9) | copy-start | bytes 1540
  0.0 12.6 %copy-start.3 = (f32[128]{0:T(128)S(1)}, f32[128]{0:T(128)}, u32[]{:S(2)}) copy-start(f32[128]{0:T(128)} %param.10) | copy-start | bytes 1540
  7.9 34.1 %copy-start.4 = (f32[8]{0:T(128)S(1)}, f32[8]{0:T(128)}, u32[]{:S(2)}) copy-start(f32[8]{0:T(128)} %param.11) | copy-start | bytes 100
  8.0 9.6 %collective-permute-start = (bf16[4,128,256]{2,1,0:T(8,128)(2,1)}, bf16[4,128,256]{2,1,0:T(8,128)(2,1)S(1)}, u32[]{:S(2)}, u32[]{:S(2)}) collective-permute-start(bf16[4,128,256]{2,1,0:T(8,128)(2,1)} %get-tuple-element.10), channel_id=1, source_target_pairs={{0,1},{1,0},{2,3},{3,2},{4,5},{5,4},{6,7},{7,6},{8,9},{9,8},{10,11... | collective-permute-start | bytes 786440 | tf_op jit(solution)/shard_map/ppermute | solution.py:127
  11.0 9.5 %collective-permute-start.7 = (bf16[4,128,256]{2,1,0:T(8,128)(2,1)}, bf16[4,128,256]{2,1,0:T(8,128)(2,1)S(1)}, u32[]{:S(2)}, u32[]{:S(2)}) collective-permute-start(bf16[4,128,256]{2,1,0:T(8,128)(2,1)} %get-tuple-element.12), channel_id=1, source_target_pairs={{0,2},{1,3},{2,0},{3,1},{4,6},{5,7},{6,4},{7,5},{8,10},{9,11},{10,... | collective-permute-start | bytes 786440 | tf_op jit(solution)/shard_map/ppermute | solution.py:127
  18.7 5.0 %collective-permute-start.1 = (bf16[2,128,256]{2,1,0:T(8,128)(2,1)S(1)}, bf16[2,128,256]{2,1,0:T(8,128)(2,1)S(1)}, u32[]{:S(2)}, u32[]{:S(2)}) collective-permute-start(bf16[2,128,256]{2,1,0:T(8,128)(2,1)S(1)} %fusion.13), channel_id=1, source_target_pairs={{0,2},{1,3},{2,0},{3,1},{4,6},{5,7},{6,4},{7,5},{8,10},{9,11},{10,... | collective-permute-start | bytes 393224 | tf_op jit(solution)/shard_map/ppermute | solution.py:127
  21.7 5.0 %collective-permute-start.8 = (bf16[2,128,256]{2,1,0:T(8,128)(2,1)S(1)}, bf16[2,128,256]{2,1,0:T(8,128)(2,1)S(1)}, u32[]{:S(2)}, u32[]{:S(2)}) collective-permute-start(bf16[2,128,256]{2,1,0:T(8,128)(2,1)S(1)} %fusion.14), channel_id=1, source_target_pairs={{0,1},{1,0},{2,3},{3,2},{4,5},{5,4},{6,7},{7,6},{8,9},{9,8},{10,11... | collective-permute-start | bytes 393224 | tf_op jit(solution)/shard_map/ppermute | solution.py:127
  23.7 11.5 %collective-permute-start.2 = (bf16[2,128,256]{2,1,0:T(8,128)(2,1)S(1)}, bf16[2,128,256]{2,1,0:T(8,128)(2,1)S(1)}, u32[]{:S(2)}, u32[]{:S(2)}) collective-permute-start(bf16[2,128,256]{2,1,0:T(8,128)(2,1)S(1)} %fusion.11), channel_id=1, source_target_pairs={{0,4},{1,5},{2,6},{3,7},{4,0},{5,1},{6,2},{7,3},{8,12},{9,13},{10,... | collective-permute-start | bytes 393224 | tf_op jit(solution)/shard_map/ppermute | solution.py:130
  26.7 10.1 %collective-permute-start.9 = (bf16[2,128,256]{2,1,0:T(8,128)(2,1)S(1)}, bf16[2,128,256]{2,1,0:T(8,128)(2,1)S(1)}, u32[]{:S(2)}, u32[]{:S(2)}) collective-permute-start(bf16[2,128,256]{2,1,0:T(8,128)(2,1)S(1)} %fusion.12), channel_id=1, source_target_pairs={{0,4},{1,5},{2,6},{3,7},{4,0},{5,1},{6,2},{7,3},{8,12},{9,13},{10,... | collective-permute-start | bytes 393224 | tf_op jit(solution)/shard_map/ppermute | solution.py:130
  35.3 5.1 %collective-permute-start.3 = (bf16[272,256]{1,0:T(8,128)(2,1)S(1)}, bf16[272,256]{1,0:T(8,128)(2,1)S(1)}, u32[]{:S(2)}, u32[]{:S(2)}) collective-permute-start(bf16[272,256]{1,0:T(8,128)(2,1)S(1)} %pad_maximum_fusion.4), channel_id=1, source_target_pairs={{0,16},{8,24},{16,0},{24,8},{1,17},{9,25},{17,1},{25,9},{2,18},{10... | collective-permute-start | bytes 417800 | tf_op jit(solution)/shard_map/ppermute | solution.py:161
  40.4 6.3 %collective-permute-start.4 = (bf16[272,512]{1,0:T(8,128)(2,1)S(1)}, bf16[272,512]{1,0:T(8,128)(2,1)S(1)}, u32[]{:S(2)}, u32[]{:S(2)}) collective-permute-start(bf16[272,512]{1,0:T(8,128)(2,1)S(1)} %pad_maximum_fusion.2), channel_id=1, source_target_pairs={{0,8},{8,0},{16,24},{24,16},{1,9},{9,1},{17,25},{25,17},{2,10},{10... | collective-permute-start | bytes 835592 | tf_op jit(solution)/shard_map/ppermute | solution.py:163
  40.5 6.1 %collective-permute-start.10 = (bf16[272,256]{1,0:T(8,128)(2,1)S(1)}, bf16[272,256]{1,0:T(8,128)(2,1)S(1)}, u32[]{:S(2)}, u32[]{:S(2)}) collective-permute-start(bf16[272,256]{1,0:T(8,128)(2,1)S(1)} %pad_maximum_fusion.5), channel_id=1, source_target_pairs={{0,16},{8,24},{16,0},{24,8},{1,17},{9,25},{17,1},{25,9},{2,18},{10... | collective-permute-start | bytes 417800 | tf_op jit(solution)/shard_map/ppermute | solution.py:161
  46.7 4.2 %collective-permute-start.11 = (bf16[272,512]{1,0:T(8,128)(2,1)S(1)}, bf16[272,512]{1,0:T(8,128)(2,1)S(1)}, u32[]{:S(2)}, u32[]{:S(2)}) collective-permute-start(bf16[272,512]{1,0:T(8,128)(2,1)S(1)} %pad_maximum_fusion.3), channel_id=1, source_target_pairs={{0,8},{8,0},{16,24},{24,16},{1,9},{9,1},{17,25},{25,17},{2,10},{10... | collective-permute-start | bytes 835592 | tf_op jit(solution)/shard_map/ppermute | solution.py:163
  47.0 9.9 %collective-permute-start.6 = (bf16[128,1024]{1,0:T(8,128)(2,1)S(1)}, bf16[128,1024]{1,0:T(8,128)(2,1)S(1)}, u32[]{:S(2)}, u32[]{:S(2)}) collective-permute-start(bf16[128,1024]{1,0:T(8,128)(2,1)S(1)} %get-tuple-element.27), channel_id=1, source_target_pairs={{0,3},{1,2},{4,7},{5,6},{10,9},{11,8},{14,13},{15,12},{16,19},{17,... | collective-permute-start | bytes 786440 | tf_op jit(solution)/shard_map/ppermute | solution.py:179
  50.3 9.2 %collective-permute-start.5 = (bf16[128,1024]{1,0:T(8,128)(2,1)S(1)}, bf16[128,1024]{1,0:T(8,128)(2,1)S(1)}, u32[]{:S(2)}, u32[]{:S(2)}) collective-permute-start(bf16[128,1024]{1,0:T(8,128)(2,1)S(1)} %get-tuple-element.27), channel_id=1, source_target_pairs={{0,1},{1,0},{2,8},{3,9},{4,5},{5,4},{6,12},{7,13},{8,2},{9,3},{10,... | collective-permute-start | bytes 786440 | tf_op jit(solution)/shard_map/ppermute | solution.py:178
  51.2 9.4 %collective-permute-start.13 = (bf16[128,1024]{1,0:T(8,128)(2,1)S(1)}, bf16[128,1024]{1,0:T(8,128)(2,1)S(1)}, u32[]{:S(2)}, u32[]{:S(2)}) collective-permute-start(bf16[128,1024]{1,0:T(8,128)(2,1)S(1)} %get-tuple-element.25), channel_id=1, source_target_pairs={{0,3},{1,2},{4,7},{5,6},{10,9},{11,8},{14,13},{15,12},{16,19},{17,... | collective-permute-start | bytes 786440 | tf_op jit(solution)/shard_map/ppermute | solution.py:179
  53.6 11.0 %collective-permute-start.12 = (bf16[128,1024]{1,0:T(8,128)(2,1)S(1)}, bf16[128,1024]{1,0:T(8,128)(2,1)S(1)}, u32[]{:S(2)}, u32[]{:S(2)}) collective-permute-start(bf16[128,1024]{1,0:T(8,128)(2,1)S(1)} %get-tuple-element.25), channel_id=1, source_target_pairs={{0,1},{1,0},{2,8},{3,9},{4,5},{5,4},{6,12},{7,13},{8,2},{9,3},{10,... | collective-permute-start | bytes 786440 | tf_op jit(solution)/shard_map/ppermute | solution.py:178

commit v3 on v2

--- a/solution.py
+++ b/solution.py
@@ -5,8 +5,11 @@
 from jax.experimental.pallas import tpu as pltpu
 from jax.sharding import PartitionSpec as P
 
+
 GROUPS = 2
 LOADS = 8
+AHEAD = 3
+VMEM_LIMIT = 24 << 20
 GAP_ROWS = 16
 
 
@@ -55,67 +58,66 @@
     return ((index >> place) << (place + 1)) | (bit << place) | (index & ((1 << place) - 1))
 
 
-def project_body(me_ref, basis_ref, pairs_ref, *refs, firsts, n_pw):
-    outs = refs[: 2 * len(firsts)]
-    basis_mem, pairs_mem, acc, sems = refs[2 * len(firsts) :]
+def project_body(me_ref, basis_ref, pairs_ref, kept_ref, sent_ref, *refs, group, first, n_pw):
+    held = len(refs) == 1
+    if held:
+        (acc,) = refs
+        basis_mem, pairs_mem = basis_ref, pairs_ref
+    else:
+        basis_mem, pairs_mem, acc, sems = refs
     step = basis_mem.shape[0] // LOADS
     spans = [pl.ds(n * step, step) for n in range(LOADS)]
     copies = [
         [
-            pltpu.make_async_copy(basis_ref.at[span], basis_mem.at[span], sems.at[0, n]),
-            pltpu.make_async_copy(pairs_ref.at[span], pairs_mem.at[span], sems.at[1, n]),
+            pltpu.make_async_copy(source.at[span], target.at[span], sems.at[k, n])
+            for k, (source, target) in enumerate([(basis_ref, basis_mem), (pairs_ref, pairs_mem)])
         ]
-        for n, span in enumerate(spans)
+        for n, span in enumerate([] if held else spans)
     ]
-    for both in copies:
-        for copy in both:
+    for copy in sum(copies[:AHEAD], []):
+        copy.start()
+    rows = acc.shape[0] // n_pw
+    columns = pl.ds(group * acc.shape[1], acc.shape[1])
+    for n, span in enumerate(spans):
+        for copy in sum(copies[n : n + 1], []):
+            copy.wait()
+        for copy in sum(copies[n + AHEAD : n + AHEAD + 1], []):
             copy.start()
-    for n, span in enumerate(spans):
-        for copy in copies[n]:
-            copy.wait()
         product = lax.dot_general(
-            basis_mem[span], pairs_mem[span], (((0,), (0,)), ((), ())),
+            basis_mem[span], pairs_mem[span, columns], (((0,), (0,)), ((), ())),
             preferred_element_type=jnp.float32,
         )
         acc[...] = product if n == 0 else acc[...] + product
-    rows = acc.shape[0] // n_pw
-    cols = acc.shape[1] // len(firsts)
-    for group, first in enumerate(firsts):
-        kept_ref, sent_ref = outs[2 * group], outs[2 * group + 1]
-        span = pl.ds(group * cols, cols)
-        bit = (me_ref[0] >> first) & 1
-        for q in range(n_pw // 2):
-            mine = pl.multiple_of(with_bit(q, bit, first) * rows, rows)
-            other = pl.multiple_of(with_bit(q, 1 - bit, first) * rows, rows)
-            kept_ref[q] = acc[pl.ds(mine, rows), span]
-            sent_ref[q] = acc[pl.ds(other, rows), span].astype(jnp.bfloat16)
-
-
-def project(basis, pair_products, me, firsts, n_pw):
-    depth, rows_all = basis.shape
-    cols_all = pair_products.shape[1]
-    shape = (n_pw // 2, rows_all // n_pw, cols_all // len(firsts))
-    outs = []
-    for _ in firsts:
-        outs += [jax.ShapeDtypeStruct(shape, jnp.float32), jax.ShapeDtypeStruct(shape, jnp.bfloat16)]
-    body = lambda *refs: project_body(*refs, firsts=firsts, n_pw=n_pw)
-    flat = pl.pallas_call(
+    bit = (me_ref[0] >> first) & 1
+    for q in range(n_pw // 2):
+        mine = pl.multiple_of(with_bit(q, bit, first) * rows, rows)
+        other = pl.multiple_of(with_bit(q, 1 - bit, first) * rows, rows)
+        kept_ref[q] = acc[pl.ds(mine, rows)]
+        sent_ref[q] = acc[pl.ds(other, rows)].astype(jnp.bfloat16)
+
+
+def project(basis, pair_products, me, group, first, n_pw):
+    _, rows_all = basis.shape
+    cols = pair_products.shape[1] // GROUPS
+    shape = (n_pw // 2, rows_all // n_pw, cols)
+    outs = [pltpu.VMEM(shape, jnp.float32), pltpu.VMEM(shape, jnp.bfloat16)]
+    scratch = [pltpu.VMEM((rows_all, cols), jnp.float32)]
+    space = pltpu.VMEM if group else pltpu.HBM
+    if not group:
+        outs += [pltpu.VMEM(a.shape, a.dtype) for a in (basis, pair_products)]
+        scratch.append(pltpu.SemaphoreType.DMA((2, LOADS)))
+        basis = pltpu.with_memory_space_constraint(basis, space)
+        pair_products = pltpu.with_memory_space_constraint(pair_products, space)
+    body = lambda *refs: project_body(*refs, group=group, first=first, n_pw=n_pw)
+    return pl.pallas_call(
         body,
-        in_specs=[
-            pl.BlockSpec(memory_space=pltpu.SMEM),
-            pl.BlockSpec(memory_space=pl.ANY),
-            pl.BlockSpec(memory_space=pl.ANY),
-        ],
+        in_specs=[pl.BlockSpec(memory_space=pltpu.SMEM)] + [pl.BlockSpec(memory_space=space)] * 2,
         out_shape=outs,
-        scratch_shapes=[
-            pltpu.VMEM(basis.shape, basis.dtype),
-            pltpu.VMEM(pair_products.shape, pair_products.dtype),
-            pltpu.VMEM((rows_all, cols_all), jnp.float32),
-            pltpu.SemaphoreType.DMA((2, LOADS)),
-        ],
+        out_specs=[pl.BlockSpec(memory_space=pltpu.VMEM)] * len(outs),
+        scratch_shapes=scratch,
+        compiler_params=pltpu.CompilerParams(vmem_limit_bytes=VMEM_LIMIT),
         name="project",
     )(me.astype(jnp.int32)[None], basis, pair_products)
-    return [(flat[2 * g], flat[2 * g + 1]) for g in range(len(firsts))]
 
 
 def sum_low_bits(kept, sent, order, n_pw, me):
@@ -124,16 +126,17 @@
         place = number - sum(g < number for g in gone)
         if gone:
             kept, sent = halves(blocks, (me >> number) & 1, place)
-        got = lax.ppermute(sent.astype(jnp.bfloat16), "pw", flip(n_pw, 1 << number))
+        sent = sent.astype(jnp.bfloat16)
+        got = lax.ppermute(sent, "pw", flip(n_pw, 1 << number))
         blocks = kept + got.astype(jnp.float32)
         gone.append(number)
-    got = lax.ppermute(blocks.astype(jnp.bfloat16), "pw", flip(n_pw, n_pw // 2))
+    sent = blocks.astype(jnp.bfloat16)
+    got = lax.ppermute(sent, "pw", flip(n_pw, n_pw // 2))
     return (blocks + got.astype(jnp.float32)).astype(jnp.bfloat16)
 
 
 def exchange(summed, gap_rows, order, n_pair, n_pw, j, me):
     blocks = summed
-    left = sorted(order)
     gone = list(order)
     for number in reversed(order):
         gone.remove(number)
@@ -153,6 +156,10 @@
     return whole[m_rows : m_rows + rows], whole[:m_rows], join_gap(whole[m_rows + rows :])
 
 
+def is_square(n_pair, n_pw):
+    return n_pair.bit_length() == 3 and n_pw.bit_length() == 4
+
+
 def exchange_square(summed, gap_rows, n_pair, n_pw, j, me):
     chip, core = j >> 1, j & 1
     far, near, side = me >> 2, (me >> 1) & 1, me & 1
@@ -161,9 +168,7 @@
     across = lax.ppermute(own, "pair", flip(n_pair, 2))
     both = jnp.concatenate([own, across], 1)
     twin = lax.ppermute(both, "pair", flip(n_pair, 1))
-    whole = jnp.concatenate(
-        [jnp.where(core == 0, both, twin), jnp.where(core == 0, twin, both)], 1
-    )
+    whole = jnp.concatenate([jnp.where(core == 0, both, twin), jnp.where(core == 0, twin, both)], 1)
     blocks = whole[: n * rows].reshape(n, rows, 2 * both.shape[1])
     rows_n = lax.dynamic_index_in_dim(blocks, far, 0, False)
     mine = lax.dynamic_index_in_dim(blocks, chip, 0, False)
@@ -203,12 +208,17 @@
         if group % 2:
             order[:2] = order[:2][::-1]
         orders.append(order)
-    partials = project(basis, pair_products, me, [order[0] for order in orders], n_pw)
+    partials = []
+    for group, order in enumerate(orders):
+        kept, sent, *held = project(basis, pair_products, me, group, order[0], n_pw)
+        if held:
+            basis, pair_products = held
+        partials.append((kept, sent))
     for group, order in enumerate(orders):
         cut = slice(group * block_size, (group + 1) * block_size)
         summed = sum_low_bits(*partials[group], order, n_pw, me)
         gap_rows = split_gap(gap[cut])
-        if n_pair.bit_length() == 3 and n_pw.bit_length() == 4:
+        if is_square(n_pair, n_pw):
             rows_n, rows_m, gaps = exchange_square(summed, gap_rows, n_pair, n_pw, j, me)
         else:
             rows_n, rows_m, gaps = exchange(summed, gap_rows, order, n_pair, n_pw, j, me)
@@ -223,6 +233,7 @@
 
 def solution(mesh):
     placed = (P("pw", "pair"), P("pw", None), P(), P(), P(), P("pair"), P("pair"))
+
     return jax.shard_map(
         per_device, mesh=mesh, in_specs=placed, out_specs=P(None, "pw", "pair"), check_vma=False
     )

time: 66.7 us -> 65.4 us (0.981)
  other arithmetic: 3.52 us -> 1.42 us
  waiting for transfers between devices: 28.4 us -> 27.1 us
  Pallas kernels: 7.93 us -> 9.21 us
    ppermute x2, waiting for transfers between devices: 2.81 us -> 0.01 us  [exchange_square(): second = lax.ppermute(mine, ('pair', 'pw'), diagonal)]
    add x2, other arithmetic: 2.19 us -> 0.11 us  [sum_low_bits(): blocks = kept + got.astype(jnp.float32)]
    pallas_call x1 -> x2, Pallas kernels: 7.93 us -> 9.21 us  [project(): pl.pallas_call(body, in_specs=[pl.BlockSpec(memory_space=pltpu.SMEM)] + [...]
    ppermute x6, waiting for transfers between devices: 10.8 us -> 11.8 us  [the longest x2 5.93 us: sum_low_bits(): got = lax.ppermute(sent, 'pw', flip(n_pw, n_pw // 2))]
    ppermute x2, starting transfers between devices: 5.71 us -> 4.76 us  [exchange_square(): second = lax.ppermute(mine, ('pair', 'pw'), diagonal)]
    ppermute x2, starting transfers between devices: 1.21 us -> 2.16 us  [exchange_square(): first = lax.ppermute(mine, ('pair', 'pw'), hop)]
  transfers between devices with their start and end apart: 14 -> 14, of which waited for: 10 -> 6; matrix products, arithmetic and copies ran while one was open for 6% -> 3% of each run, Pallas kernels for 0% -> 0%
where the time goes in v3:
time: 65.4 us; the launch traced here: 64.6 us
  waiting for transfers between devices  27.1 us (41%)
  starting transfers between devices  23.9 us (37%)
  Pallas kernels  9.21 us (14%)
  matrix products  2.49 us (4%)
  other arithmetic  1.42 us (2%)
    pallas_call x2, Pallas kernels, project(): pl.pallas_call(body, in_specs=[pl.BlockSpec(memory_space=pltpu.SMEM)] + [...  9.21 us
    ppermute x2, waiting for transfers between devices, exchange_square(): across = lax.ppermute(own, 'pair', flip(n_pair, 2))  8.08 us
    ppermute x4, starting transfers between devices, sum_low_bits(): got = lax.ppermute(sent, 'pw', flip(n_pw, 1 << number))  8.03 us
    ppermute x2, waiting for transfers between devices, exchange_square(): first = lax.ppermute(mine, ('pair', 'pw'), hop)  7.21 us
    ppermute x2, waiting for transfers between devices, sum_low_bits(): got = lax.ppermute(sent, 'pw', flip(n_pw, n_pw // 2))  5.93 us
    ppermute x4, waiting for transfers between devices, sum_low_bits(): got = lax.ppermute(sent, 'pw', flip(n_pw, 1 << number))  5.84 us
    ppermute x2, starting transfers between devices, sum_low_bits(): got = lax.ppermute(sent, 'pw', flip(n_pw, n_pw // 2))  5.71 us
    ppermute x2, starting transfers between devices, exchange_square(): second = lax.ppermute(mine, ('pair', 'pw'), diagonal)  4.76 us
  transfers between devices with their start and end apart: 14, of which 6 were waited for; matrix products, arithmetic and copies ran while one was open for 3% of the time, Pallas kernels for 0%

profile of v3, /device:TPU:0, one launch (start us, length us, event | category | flops | bytes accessed | tf_op | source)
XLA Modules:
  0.0 64.6 jit_solution(9884254199892070341)
XLA Ops:
  0.0 6.6 %project.2 = (f32[4,128,256]{2,1,0:T(8,128)S(1)}, bf16[4,128,256]{2,1,0:T(8,128)(2,1)S(1)}, bf16[4096,1024]{1,0:T(8,128)(2,1)S(1)}, bf16[4096,512]{1,0:T(8,128)(2,1)S(1)}) custom-call(s32[1]{0:T(128)} %bitcast.refs_0_, bf16[4096,1024]{1,0:T(8,128)(2,1)} %refs_1_.1, bf16[4096,512]{1,0:T(8,128)(2,1)} %refs_2_.1), custom_call_target="tpu_custom_call" | custom-call | tf_op jit(solution)/shard_map/project/pallas_call | solution.py:112
  6.6 0.0 copy-start
  6.7 0.0 copy-start.1
  6.7 0.0 copy-start.2
  6.7 0.0 copy-start.3
  6.7 2.6 %project.3 = (f32[4,128,256]{2,1,0:T(8,128)S(1)}, bf16[4,128,256]{2,1,0:T(8,128)(2,1)S(1)}) custom-call(s32[1]{0:T(128)} %bitcast.refs_0_, bf16[4096,1024]{1,0:T(8,128)(2,1)S(1)} %get-tuple-element.13.refs_1_, bf16[4096,512]{1,0:T(8,128)(2,1)S(1)} %get-tuple-element.14.refs_2_), custom_call_target="tpu_custom_call" | custom-call | tf_op jit(solution)/shard_map/project/pallas_call | solution.py:112
  9.3 0.0 copy-start.4
  9.3 3.1 %collective-permute-start.7 = (bf16[4,128,256]{2,1,0:T(8,128)(2,1)S(1)}, bf16[4,128,256]{2,1,0:T(8,128)(2,1)S(1)}, u32[]{:S(2)}, u32[]{:S(2)}) collective-permute-start(bf16[4,128,256]{2,1,0:T(8,128)(2,1)S(1)} %get-tuple-element.16), channel_id=1, source_target_pairs={{0,2},{1,3},{2,0},{3,1},{4,6},{5,7},{6,4},{7,5},{8,10},{9,11},{10,... | collective-permute-start | bytes 786440 | tf_op jit(solution)/shard_map/ppermute | solution.py:130
  12.4 1.5 %collective-permute-start = (bf16[4,128,256]{2,1,0:T(8,128)(2,1)S(1)}, bf16[4,128,256]{2,1,0:T(8,128)(2,1)S(1)}, u32[]{:S(2)}, u32[]{:S(2)}) collective-permute-start(bf16[4,128,256]{2,1,0:T(8,128)(2,1)S(1)} %get-tuple-element.12), channel_id=1, source_target_pairs={{0,1},{1,0},{2,3},{3,2},{4,5},{5,4},{6,7},{7,6},{8,9},{9,8},{10,11... | collective-permute-start | bytes 786440 | tf_op jit(solution)/shard_map/ppermute | solution.py:130
  13.9 0.0 copy-done
  13.9 0.0 copy-done.1
  13.9 0.0 copy-done.2
  13.9 0.0 copy-done.3
  13.9 0.4 select_reduce_fusion
  14.4 4.3 %collective-permute-done.7 = bf16[4,128,256]{2,1,0:T(8,128)(2,1)S(1)} collective-permute-done((bf16[4,128,256]{2,1,0:T(8,128)(2,1)S(1)}, bf16[4,128,256]{2,1,0:T(8,128)(2,1)S(1)}, u32[]{:S(2)}, u32[]{:S(2)}) %collective-permute-start.7) | collective-permute-done | bytes 262176 | tf_op jit(solution)/shard_map/ppermute | solution.py:130
  18.7 0.1 convert_add_fusion
  18.8 1.7 %collective-permute-start.8 = (bf16[2,128,256]{2,1,0:T(8,128)(2,1)S(1)}, bf16[2,128,256]{2,1,0:T(8,128)(2,1)S(1)}, u32[]{:S(2)}, u32[]{:S(2)}) collective-permute-start(bf16[2,128,256]{2,1,0:T(8,128)(2,1)S(1)} %fusion.14), channel_id=1, source_target_pairs={{0,1},{1,0},{2,3},{3,2},{4,5},{5,4},{6,7},{7,6},{8,9},{9,8},{10,11... | collective-permute-start | bytes 393224 | tf_op jit(solution)/shard_map/ppermute | solution.py:130
  20.6 0.0 collective-permute-done
  20.6 0.1 convert_add_fusion.1
  20.6 1.6 %collective-permute-start.1 = (bf16[2,128,256]{2,1,0:T(8,128)(2,1)S(1)}, bf16[2,128,256]{2,1,0:T(8,128)(2,1)S(1)}, u32[]{:S(2)}, u32[]{:S(2)}) collective-permute-start(bf16[2,128,256]{2,1,0:T(8,128)(2,1)S(1)} %fusion.13), channel_id=1, source_target_pairs={{0,2},{1,3},{2,0},{3,1},{4,6},{5,7},{6,4},{7,5},{8,10},{9,11},{10,... | collective-permute-start | bytes 393224 | tf_op jit(solution)/shard_map/ppermute | solution.py:130
  22.3 1.5 %collective-permute-done.8 = bf16[2,128,256]{2,1,0:T(8,128)(2,1)S(1)} collective-permute-done((bf16[2,128,256]{2,1,0:T(8,128)(2,1)S(1)}, bf16[2,128,256]{2,1,0:T(8,128)(2,1)S(1)}, u32[]{:S(2)}, u32[]{:S(2)}) %collective-permute-start.8) | collective-permute-done | bytes 131104 | tf_op jit(solution)/shard_map/ppermute | solution.py:130
  23.9 2.8 %collective-permute-start.9 = (bf16[2,128,256]{2,1,0:T(8,128)(2,1)S(1)}, bf16[2,128,256]{2,1,0:T(8,128)(2,1)S(1)}, u32[]{:S(2)}, u32[]{:S(2)}) collective-permute-start(bf16[2,128,256]{2,1,0:T(8,128)(2,1)S(1)} %fusion.12), channel_id=1, source_target_pairs={{0,4},{1,5},{2,6},{3,7},{4,0},{5,1},{6,2},{7,3},{8,12},{9,13},{10,... | collective-permute-start | bytes 393224 | tf_op jit(solution)/shard_map/ppermute | solution.py:134
  26.7 0.0 collective-permute-done.1
  26.7 2.9 %collective-permute-start.2 = (bf16[2,128,256]{2,1,0:T(8,128)(2,1)S(1)}, bf16[2,128,256]{2,1,0:T(8,128)(2,1)S(1)}, u32[]{:S(2)}, u32[]{:S(2)}) collective-permute-start(bf16[2,128,256]{2,1,0:T(8,128)(2,1)S(1)} %fusion.11), channel_id=1, source_target_pairs={{0,4},{1,5},{2,6},{3,7},{4,0},{5,1},{6,2},{7,3},{8,12},{9,13},{10,... | collective-permute-start | bytes 393224 | tf_op jit(solution)/shard_map/ppermute | solution.py:134
  29.6 5.9 %collective-permute-done.9 = bf16[2,128,256]{2,1,0:T(8,128)(2,1)S(1)} collective-permute-done((bf16[2,128,256]{2,1,0:T(8,128)(2,1)S(1)}, bf16[2,128,256]{2,1,0:T(8,128)(2,1)S(1)}, u32[]{:S(2)}, u32[]{:S(2)}) %collective-permute-start.9) | collective-permute-done | bytes 131104 | tf_op jit(solution)/shard_map/ppermute | solution.py:134
  35.6 0.1 add_convert_fusion
  35.6 1.6 %collective-permute-start.10 = (bf16[272,256]{1,0:T(8,128)(2,1)S(1)}, bf16[272,256]{1,0:T(8,128)(2,1)S(1)}, u32[]{:S(2)}, u32[]{:S(2)}) collective-permute-start(bf16[272,256]{1,0:T(8,128)(2,1)S(1)} %pad_maximum_fusion.5), channel_id=1, source_target_pairs={{0,16},{8,24},{16,0},{24,8},{1,17},{9,25},{17,1},{25,9},{2,18},{10... | collective-permute-start | bytes 417800 | tf_op jit(solution)/shard_map/ppermute | solution.py:168
  37.2 0.0 collective-permute-done.2
  37.2 0.1 add_convert_fusion.1
  37.2 3.5 %collective-permute-done.10 = bf16[272,256]{1,0:T(8,128)(2,1)S(1)} collective-permute-done((bf16[272,256]{1,0:T(8,128)(2,1)S(1)}, bf16[272,256]{1,0:T(8,128)(2,1)S(1)}, u32[]{:S(2)}, u32[]{:S(2)}) %collective-permute-start.10) | collective-permute-done | bytes 139296 | tf_op jit(solution)/shard_map/ppermute | solution.py:168
  40.8 0.1 collective-permute-start.11
  40.9 1.6 %collective-permute-start.3 = (bf16[272,256]{1,0:T(8,128)(2,1)S(1)}, bf16[272,256]{1,0:T(8,128)(2,1)S(1)}, u32[]{:S(2)}, u32[]{:S(2)}) collective-permute-start(bf16[272,256]{1,0:T(8,128)(2,1)S(1)} %pad_maximum_fusion.4), channel_id=1, source_target_pairs={{0,16},{8,24},{16,0},{24,8},{1,17},{9,25},{17,1},{25,9},{2,18},{10... | collective-permute-start | bytes 417800 | tf_op jit(solution)/shard_map/ppermute | solution.py:168
  42.4 0.0 copy-done.4
  42.4 4.6 %collective-permute-done.3 = bf16[272,256]{1,0:T(8,128)(2,1)S(1)} collective-permute-done((bf16[272,256]{1,0:T(8,128)(2,1)S(1)}, bf16[272,256]{1,0:T(8,128)(2,1)S(1)}, u32[]{:S(2)}, u32[]{:S(2)}) %collective-permute-start.3) | collective-permute-done | bytes 139296 | tf_op jit(solution)/shard_map/ppermute | solution.py:168
  47.0 0.1 collective-permute-start.4
  47.1 0.0 collective-permute-done.11
  47.1 0.1 broadcast_select_fusion.1
  47.2 0.1 pad_maximum_fusion
  47.3 0.1 dynamic-slice_bitcast_fusion
  47.4 1.6 %collective-permute-start.12 = (bf16[128,1024]{1,0:T(8,128)(2,1)S(1)}, bf16[128,1024]{1,0:T(8,128)(2,1)S(1)}, u32[]{:S(2)}, u32[]{:S(2)}) collective-permute-start(bf16[128,1024]{1,0:T(8,128)(2,1)S(1)} %get-tuple-element.29), channel_id=1, source_target_pairs={{0,1},{1,0},{2,8},{3,9},{4,5},{5,4},{6,12},{7,13},{8,2},{9,3},{10,... | collective-permute-start | bytes 786440 | tf_op jit(solution)/shard_map/ppermute | solution.py:183
  49.0 3.5 %collective-permute-start.13 = (bf16[128,1024]{1,0:T(8,128)(2,1)S(1)}, bf16[128,1024]{1,0:T(8,128)(2,1)S(1)}, u32[]{:S(2)}, u32[]{:S(2)}) collective-permute-start(bf16[128,1024]{1,0:T(8,128)(2,1)S(1)} %get-tuple-element.29), channel_id=1, source_target_pairs={{0,3},{1,2},{4,7},{5,6},{10,9},{11,8},{14,13},{15,12},{16,19},{17,... | collective-permute-start | bytes 786440 | tf_op jit(solution)/shard_map/ppermute | solution.py:184
  52.4 0.0 collective-permute-done.4
  52.4 0.1 broadcast_select_fusion.3
  52.5 0.1 pad_maximum_fusion.1
  52.6 0.1 dynamic-slice_bitcast_fusion.1
  52.7 0.6 collective-permute-start.5
  53.2 1.3 %collective-permute-start.6 = (bf16[128,1024]{1,0:T(8,128)(2,1)S(1)}, bf16[128,1024]{1,0:T(8,128)(2,1)S(1)}, u32[]{:S(2)}, u32[]{:S(2)}) collective-permute-start(bf16[128,1024]{1,0:T(8,128)(2,1)S(1)} %get-tuple-element.31), channel_id=1, source_target_pairs={{0,3},{1,2},{4,7},{5,6},{10,9},{11,8},{14,13},{15,12},{16,19},{17,... | collective-permute-start | bytes 786440 | tf_op jit(solution)/shard_map/ppermute | solution.py:184
  54.6 0.1 divide_multiply_fusion
  54.7 7.2 %collective-permute-done.5 = bf16[128,1024]{1,0:T(8,128)(2,1)S(1)} collective-permute-done((bf16[128,1024]{1,0:T(8,128)(2,1)S(1)}, bf16[128,1024]{1,0:T(8,128)(2,1)S(1)}, u32[]{:S(2)}, u32[]{:S(2)}) %collective-permute-start.5) | collective-permute-done | bytes 262176 | tf_op jit(solution)/shard_map/ppermute | solution.py:183
  61.9 0.0 collective-permute-done.6
  62.0 0.8 %fusion = f32[8,128,256]{2,1,0:T(8,128)S(1)} fusion(f32[128,1024]{1,0:T(8,128)S(1)} %get-tuple-element.32, f32[8,1024]{1,0:T(8,128)S(1)} %get-tuple-element.40, bf16[128,1024]{1,0:T(8,128)(2,1)S(1)} %get-tuple-element.24, bf16[128,1024]{1,0:T(8,128)(2,1)S(1)} %get-tuple-element.23), kind=kOutput, calls=%fused_computation.2 | convolution fusion | flops 540016640 | bytes 2129920 | tf_op jit(solution)/shard_map/kpc,nc->kpn/dot_general | solution.py:229
  62.7 0.0 collective-permute-done.12
  62.8 0.0 collective-permute-done.13
  62.8 0.1 broadcast_select_fusion.9
  62.8 1.7 %fusion.6 = f32[8,128,256]{2,1,0:T(8,128)} fusion(f32[8,128,256]{2,1,0:T(8,128)S(1)} %fusion, f32[128,1024]{1,0:T(8,128)S(1)} %get-tuple-element.30, f32[8,1024]{1,0:T(8,128)S(1)} %get-tuple-element.39, bf16[128,1024]{1,0:T(8,128)(2,1)S(1)} %get-tuple-element.22, bf16[128,1024]{1,0:T(8,128)(2,1)S(1)} %get-tuple-element.21), kind=kOutput, calls=%fused_computation.8 | convolution fusion | flops 540278784 | bytes 3178496 | tf_op jit(solution)/shard_map/kpc,nc->kpn/dot_general | solution.py:229
  (24 shorter events, 0.3 us)
Async XLA Ops:
  6.6 7.3 %copy-start = (s32[512]{0:T(512)S(1)}, s32[512]{0:T(512)}, u32[]{:S(2)}) copy-start(s32[512]{0:T(512)} %param.12) | copy-start | bytes 6148
  6.7 7.3 %copy-start.1 = (s32[512]{0:T(512)S(1)}, s32[512]{0:T(512)}, u32[]{:S(2)}) copy-start(s32[512]{0:T(512)} %param.13) | copy-start | bytes 6148
  6.7 7.3 %copy-start.2 = (f32[128]{0:T(128)S(1)}, f32[128]{0:T(128)}, u32[]{:S(2)}) copy-start(f32[128]{0:T(128)} %param.9) | copy-start | bytes 1540
  6.7 7.3 %copy-start.3 = (f32[128]{0:T(128)S(1)}, f32[128]{0:T(128)}, u32[]{:S(2)}) copy-start(f32[128]{0:T(128)} %param.10) | copy-start | bytes 1540
  9.3 33.2 %copy-start.4 = (f32[8]{0:T(128)S(1)}, f32[8]{0:T(128)}, u32[]{:S(2)}) copy-start(f32[8]{0:T(128)} %param.11) | copy-start | bytes 100
  9.3 9.4 %collective-permute-start.7 = (bf16[4,128,256]{2,1,0:T(8,128)(2,1)S(1)}, bf16[4,128,256]{2,1,0:T(8,128)(2,1)S(1)}, u32[]{:S(2)}, u32[]{:S(2)}) collective-permute-start(bf16[4,128,256]{2,1,0:T(8,128)(2,1)S(1)} %get-tuple-element.16), channel_id=1, source_target_pairs={{0,2},{1,3},{2,0},{3,1},{4,6},{5,7},{6,4},{7,5},{8,10},{9,11},{10,... | collective-permute-start | bytes 786440 | tf_op jit(solution)/shard_map/ppermute | solution.py:130
  12.4 8.1 %collective-permute-start = (bf16[4,128,256]{2,1,0:T(8,128)(2,1)S(1)}, bf16[4,128,256]{2,1,0:T(8,128)(2,1)S(1)}, u32[]{:S(2)}, u32[]{:S(2)}) collective-permute-start(bf16[4,128,256]{2,1,0:T(8,128)(2,1)S(1)} %get-tuple-element.12), channel_id=1, source_target_pairs={{0,1},{1,0},{2,3},{3,2},{4,5},{5,4},{6,7},{7,6},{8,9},{9,8},{10,11... | collective-permute-start | bytes 786440 | tf_op jit(solution)/shard_map/ppermute | solution.py:130
  18.8 5.0 %collective-permute-start.8 = (bf16[2,128,256]{2,1,0:T(8,128)(2,1)S(1)}, bf16[2,128,256]{2,1,0:T(8,128)(2,1)S(1)}, u32[]{:S(2)}, u32[]{:S(2)}) collective-permute-start(bf16[2,128,256]{2,1,0:T(8,128)(2,1)S(1)} %fusion.14), channel_id=1, source_target_pairs={{0,1},{1,0},{2,3},{3,2},{4,5},{5,4},{6,7},{7,6},{8,9},{9,8},{10,11... | collective-permute-start | bytes 393224 | tf_op jit(solution)/shard_map/ppermute | solution.py:130
  20.6 6.1 %collective-permute-start.1 = (bf16[2,128,256]{2,1,0:T(8,128)(2,1)S(1)}, bf16[2,128,256]{2,1,0:T(8,128)(2,1)S(1)}, u32[]{:S(2)}, u32[]{:S(2)}) collective-permute-start(bf16[2,128,256]{2,1,0:T(8,128)(2,1)S(1)} %fusion.13), channel_id=1, source_target_pairs={{0,2},{1,3},{2,0},{3,1},{4,6},{5,7},{6,4},{7,5},{8,10},{9,11},{10,... | collective-permute-start | bytes 393224 | tf_op jit(solution)/shard_map/ppermute | solution.py:130
  23.9 11.7 %collective-permute-start.9 = (bf16[2,128,256]{2,1,0:T(8,128)(2,1)S(1)}, bf16[2,128,256]{2,1,0:T(8,128)(2,1)S(1)}, u32[]{:S(2)}, u32[]{:S(2)}) collective-permute-start(bf16[2,128,256]{2,1,0:T(8,128)(2,1)S(1)} %fusion.12), channel_id=1, source_target_pairs={{0,4},{1,5},{2,6},{3,7},{4,0},{5,1},{6,2},{7,3},{8,12},{9,13},{10,... | collective-permute-start | bytes 393224 | tf_op jit(solution)/shard_map/ppermute | solution.py:134
  26.7 10.4 %collective-permute-start.2 = (bf16[2,128,256]{2,1,0:T(8,128)(2,1)S(1)}, bf16[2,128,256]{2,1,0:T(8,128)(2,1)S(1)}, u32[]{:S(2)}, u32[]{:S(2)}) collective-permute-start(bf16[2,128,256]{2,1,0:T(8,128)(2,1)S(1)} %fusion.11), channel_id=1, source_target_pairs={{0,4},{1,5},{2,6},{3,7},{4,0},{5,1},{6,2},{7,3},{8,12},{9,13},{10,... | collective-permute-start | bytes 393224 | tf_op jit(solution)/shard_map/ppermute | solution.py:134
  35.6 5.1 %collective-permute-start.10 = (bf16[272,256]{1,0:T(8,128)(2,1)S(1)}, bf16[272,256]{1,0:T(8,128)(2,1)S(1)}, u32[]{:S(2)}, u32[]{:S(2)}) collective-permute-start(bf16[272,256]{1,0:T(8,128)(2,1)S(1)} %pad_maximum_fusion.5), channel_id=1, source_target_pairs={{0,16},{8,24},{16,0},{24,8},{1,17},{9,25},{17,1},{25,9},{2,18},{10... | collective-permute-start | bytes 417800 | tf_op jit(solution)/shard_map/ppermute | solution.py:168
  40.8 6.3 %collective-permute-start.11 = (bf16[272,512]{1,0:T(8,128)(2,1)S(1)}, bf16[272,512]{1,0:T(8,128)(2,1)S(1)}, u32[]{:S(2)}, u32[]{:S(2)}) collective-permute-start(bf16[272,512]{1,0:T(8,128)(2,1)S(1)} %pad_maximum_fusion.3), channel_id=1, source_target_pairs={{0,8},{8,0},{16,24},{24,16},{1,9},{9,1},{17,25},{25,17},{2,10},{10... | collective-permute-start | bytes 835592 | tf_op jit(solution)/shard_map/ppermute | solution.py:170
  40.9 6.1 %collective-permute-start.3 = (bf16[272,256]{1,0:T(8,128)(2,1)S(1)}, bf16[272,256]{1,0:T(8,128)(2,1)S(1)}, u32[]{:S(2)}, u32[]{:S(2)}) collective-permute-start(bf16[272,256]{1,0:T(8,128)(2,1)S(1)} %pad_maximum_fusion.4), channel_id=1, source_target_pairs={{0,16},{8,24},{16,0},{24,8},{1,17},{9,25},{17,1},{25,9},{2,18},{10... | collective-permute-start | bytes 417800 | tf_op jit(solution)/shard_map/ppermute | solution.py:168
  47.0 5.4 %collective-permute-start.4 = (bf16[272,512]{1,0:T(8,128)(2,1)S(1)}, bf16[272,512]{1,0:T(8,128)(2,1)S(1)}, u32[]{:S(2)}, u32[]{:S(2)}) collective-permute-start(bf16[272,512]{1,0:T(8,128)(2,1)S(1)} %pad_maximum_fusion.2), channel_id=1, source_target_pairs={{0,8},{8,0},{16,24},{24,16},{1,9},{9,1},{17,25},{25,17},{2,10},{10... | collective-permute-start | bytes 835592 | tf_op jit(solution)/shard_map/ppermute | solution.py:170
  47.4 15.4 %collective-permute-start.12 = (bf16[128,1024]{1,0:T(8,128)(2,1)S(1)}, bf16[128,1024]{1,0:T(8,128)(2,1)S(1)}, u32[]{:S(2)}, u32[]{:S(2)}) collective-permute-start(bf16[128,1024]{1,0:T(8,128)(2,1)S(1)} %get-tuple-element.29), channel_id=1, source_target_pairs={{0,1},{1,0},{2,8},{3,9},{4,5},{5,4},{6,12},{7,13},{8,2},{9,3},{10,... | collective-permute-start | bytes 786440 | tf_op jit(solution)/shard_map/ppermute | solution.py:183
  49.0 13.8 %collective-permute-start.13 = (bf16[128,1024]{1,0:T(8,128)(2,1)S(1)}, bf16[128,1024]{1,0:T(8,128)(2,1)S(1)}, u32[]{:S(2)}, u32[]{:S(2)}) collective-permute-start(bf16[128,1024]{1,0:T(8,128)(2,1)S(1)} %get-tuple-element.29), channel_id=1, source_target_pairs={{0,3},{1,2},{4,7},{5,6},{10,9},{11,8},{14,13},{15,12},{16,19},{17,... | collective-permute-start | bytes 786440 | tf_op jit(solution)/shard_map/ppermute | solution.py:184
  52.7 9.2 %collective-permute-start.5 = (bf16[128,1024]{1,0:T(8,128)(2,1)S(1)}, bf16[128,1024]{1,0:T(8,128)(2,1)S(1)}, u32[]{:S(2)}, u32[]{:S(2)}) collective-permute-start(bf16[128,1024]{1,0:T(8,128)(2,1)S(1)} %get-tuple-element.31), channel_id=1, source_target_pairs={{0,1},{1,0},{2,8},{3,9},{4,5},{5,4},{6,12},{7,13},{8,2},{9,3},{10,... | collective-permute-start | bytes 786440 | tf_op jit(solution)/shard_map/ppermute | solution.py:183
  53.2 8.7 %collective-permute-start.6 = (bf16[128,1024]{1,0:T(8,128)(2,1)S(1)}, bf16[128,1024]{1,0:T(8,128)(2,1)S(1)}, u32[]{:S(2)}, u32[]{:S(2)}) collective-permute-start(bf16[128,1024]{1,0:T(8,128)(2,1)S(1)} %get-tuple-element.31), channel_id=1, source_target_pairs={{0,3},{1,2},{4,7},{5,6},{10,9},{11,8},{14,13},{15,12},{16,19},{17,... | collective-permute-start | bytes 786440 | tf_op jit(solution)/shard_map/ppermute | solution.py:184

commit v4 on v3

--- a/solution.py
+++ b/solution.py
@@ -7,6 +7,7 @@
 
 
 GROUPS = 2
+DIRECT = (0, 1)
 LOADS = 8
 AHEAD = 3
 VMEM_LIMIT = 24 << 20
@@ -58,7 +59,9 @@
     return ((index >> place) << (place + 1)) | (bit << place) | (index & ((1 << place) - 1))
 
 
-def project_body(me_ref, basis_ref, pairs_ref, kept_ref, sent_ref, *refs, group, first, n_pw):
+def project_body(me_ref, basis_ref, pairs_ref, *refs, group, picks, n_pw):
+    kept_ref, *sent_refs = refs[: len(picks)]
+    refs = refs[len(picks) :]
     held = len(refs) == 1
     if held:
         (acc,) = refs
@@ -88,19 +91,17 @@
             preferred_element_type=jnp.float32,
         )
         acc[...] = product if n == 0 else acc[...] + product
-    bit = (me_ref[0] >> first) & 1
-    for q in range(n_pw // 2):
-        mine = pl.multiple_of(with_bit(q, bit, first) * rows, rows)
-        other = pl.multiple_of(with_bit(q, 1 - bit, first) * rows, rows)
-        kept_ref[q] = acc[pl.ds(mine, rows)]
-        sent_ref[q] = acc[pl.ds(other, rows)].astype(jnp.bfloat16)
-
-
-def project(basis, pair_products, me, group, first, n_pw):
+    for q in range(kept_ref.shape[0]):
+        for pick, out_ref in zip(picks, [kept_ref] + sent_refs):
+            start = pl.multiple_of(pick(q, me_ref[0]) * rows, rows)
+            out_ref[q] = acc[pl.ds(start, rows)].astype(out_ref.dtype)
+
+
+def project(basis, pair_products, me, group, picks, left, n_pw):
     _, rows_all = basis.shape
     cols = pair_products.shape[1] // GROUPS
-    shape = (n_pw // 2, rows_all // n_pw, cols)
-    outs = [pltpu.VMEM(shape, jnp.float32), pltpu.VMEM(shape, jnp.bfloat16)]
+    shape = (left, rows_all // n_pw, cols)
+    outs = [pltpu.VMEM(shape, jnp.bfloat16 if n else jnp.float32) for n in range(len(picks))]
     scratch = [pltpu.VMEM((rows_all, cols), jnp.float32)]
     space = pltpu.VMEM if group else pltpu.HBM
     if not group:
@@ -108,7 +109,7 @@
         scratch.append(pltpu.SemaphoreType.DMA((2, LOADS)))
         basis = pltpu.with_memory_space_constraint(basis, space)
         pair_products = pltpu.with_memory_space_constraint(pair_products, space)
-    body = lambda *refs: project_body(*refs, group=group, first=first, n_pw=n_pw)
+    body = lambda *refs: project_body(*refs, group=group, picks=picks, n_pw=n_pw)
     return pl.pallas_call(
         body,
         in_specs=[pl.BlockSpec(memory_space=pltpu.SMEM)] + [pl.BlockSpec(memory_space=space)] * 2,
@@ -154,6 +155,16 @@
     whole = jnp.concatenate(parts, 1)
     m_rows = tiles.shape[1]
     return whole[m_rows : m_rows + rows], whole[:m_rows], join_gap(whole[m_rows + rows :])
+
+
+def sum_direct(kept, *sent, n_pw):
+    blocks = kept
+    for d, block in enumerate(sent, 1):
+        got = lax.ppermute(block, "pw", flip(n_pw, d))
+        blocks = blocks + got.astype(jnp.float32)
+    sent = blocks.astype(jnp.bfloat16)
+    got = lax.ppermute(sent, "pw", flip(n_pw, n_pw // 2))
+    return (blocks + got.astype(jnp.float32)).astype(jnp.bfloat16)
 
 
 def is_square(n_pair, n_pw):
@@ -180,6 +191,7 @@
                 diagonal.append((a * n_pw + b, a * n_pw + (b ^ 3)))
             else:
                 hop.append((a * n_pw + b, (a ^ 1) * n_pw + (b ^ 2)))
+                diagonal.append((a * n_pw + b, (a ^ 1) * n_pw + b))
     first = lax.ppermute(mine, ("pair", "pw"), hop)
     second = lax.ppermute(mine, ("pair", "pw"), diagonal)
     here = core == near
@@ -209,14 +221,27 @@
             order[:2] = order[:2][::-1]
         orders.append(order)
     partials = []
+    direct = DIRECT if is_square(n_pair, n_pw) else ()
     for group, order in enumerate(orders):
-        kept, sent, *held = project(basis, pair_products, me, group, order[0], n_pw)
-        if held:
-            basis, pair_products = held
-        partials.append((kept, sent))
+        if group in direct:
+            low = n_pw // 2
+            picks = [lambda q, i, d=d: q * low + ((i & (low - 1)) ^ d) for d in range(low)]
+            left = 2
+        else:
+            picks = [
+                lambda q, i, d=d, p=order[0]: with_bit(q, ((i >> p) & 1) ^ d, p)
+                for d in range(2)
+            ]
+            left = n_pw // 2
+        outs = project(basis, pair_products, me, group, picks, left, n_pw)
+        partials.append(outs[: len(picks)])
+        basis, pair_products = outs[len(picks) :] or (basis, pair_products)
     for group, order in enumerate(orders):
         cut = slice(group * block_size, (group + 1) * block_size)
-        summed = sum_low_bits(*partials[group], order, n_pw, me)
+        if group in direct:
+            summed = sum_direct(*partials[group], n_pw=n_pw)
+        else:
+            summed = sum_low_bits(*partials[group], order, n_pw, me)
         gap_rows = split_gap(gap[cut])
         if is_square(n_pair, n_pw):
             rows_n, rows_m, gaps = exchange_square(summed, gap_rows, n_pair, n_pw, j, me)

time: 65.4 us -> 60.6 us (0.927)
  the two profiles are of different devices: /device:TPU:0 before, /device:TPU:1 now
where the time goes in v4:
time: 60.6 us; the launch traced here: 60.5 us
  waiting for transfers between devices  24.8 us (41%)
  starting transfers between devices  22.2 us (37%)
  Pallas kernels  9.17 us (15%)
  matrix products  2.48 us (4%)
  other arithmetic  1.45 us (2%)
    ppermute x2, waiting for transfers between devices, exchange_square(): first = lax.ppermute(mine, ('pair', 'pw'), hop)  9.17 us
    pallas_call x2, Pallas kernels, project(): pl.pallas_call(body, in_specs=[pl.BlockSpec(memory_space=pltpu.SMEM)] + [...  9.17 us
    ppermute x6, starting transfers between devices, sum_direct(): got = lax.ppermute(block, 'pw', flip(n_pw, d))  8.01 us
    ppermute x2, waiting for transfers between devices, sum_direct(): got = lax.ppermute(sent, 'pw', flip(n_pw, n_pw // 2))  6.48 us
    ppermute x2, starting transfers between devices, sum_direct(): got = lax.ppermute(sent, 'pw', flip(n_pw, n_pw // 2))  5.81 us
    ppermute x2, waiting for transfers between devices, exchange_square(): across = lax.ppermute(own, 'pair', flip(n_pair, 2))  4 us
    ppermute x6, waiting for transfers between devices, sum_direct(): got = lax.ppermute(block, 'pw', flip(n_pw, d))  3.08 us
    ppermute x2, starting transfers between devices, exchange_square(): across = lax.ppermute(own, 'pair', flip(n_pair, 2))  2.55 us
  transfers between devices with their start and end apart: 16, of which 6 were waited for; matrix products, arithmetic and copies ran while one was open for 4% of the time, Pallas kernels for 0%

profile of v4, /device:TPU:1, one launch (start us, length us, event | category | flops | bytes accessed | tf_op | source)
XLA Modules:
  0.0 60.5 jit_solution(3314101072431752269)
XLA Ops:
  0.0 6.6 %project.2 = (f32[2,128,256]{2,1,0:T(8,128)S(1)}, bf16[2,128,256]{2,1,0:T(8,128)(2,1)S(1)}, bf16[2,128,256]{2,1,0:T(8,128)(2,1)S(1)}, bf16[2,128,256]{2,1,0:T(8,...) custom-call(s32[1]{0:T(128)} %bitcast.refs_0_, bf16[4096,1024]{1,0:T(8,128)(2,1)} %refs_1_.1, ...), custom_call_target="tpu_custom_call" | custom-call | tf_op jit(solution)/shard_map/project/pallas_call | solution.py:113
  6.6 0.0 copy-start
  6.6 0.0 copy-start.1
  6.6 0.0 copy-start.2
  6.7 0.0 copy-start.3
  6.7 2.6 %project.3 = (f32[2,128,256]{2,1,0:T(8,128)S(1)}, bf16[2,128,256]{2,1,0:T(8,128)(2,1)S(1)}, bf16[2,128,256]{2,1,0:T(8,128)(2,1)S(1)}, bf16[2,128,256]{2,1,0:T(8,128)(2,1)S(1)}) custom-call(s32[1]{0:T(128)} %bitcast.refs_0_, bf16[4096,1024]{1,0:T(8,128)(2,1)S(1)} %get-tuple-element.19.refs_1_, bf16[4096,512]{1,0:T(8,128)(2,1)S(1)} %get-tuple-element.20.refs_2_), custom_call_target="tpu_custom_call" | custom-call | tf_op jit(solution)/shard_map/project/pallas_call | solution.py:113
  9.2 0.0 copy-start.4
  9.2 3.2 %collective-permute-start.10 = (bf16[2,128,256]{2,1,0:T(8,128)(2,1)S(1)}, bf16[2,128,256]{2,1,0:T(8,128)(2,1)S(1)}, u32[]{:S(2)}, u32[]{:S(2)}) collective-permute-start(bf16[2,128,256]{2,1,0:T(8,128)(2,1)S(1)} %get-tuple-element.24), channel_id=1, source_target_pairs={{0,3},{1,2},{2,1},{3,0},{4,7},{5,6},{6,5},{7,4},{8,11},{9,10},{10,... | collective-permute-start | bytes 393224 | tf_op jit(solution)/shard_map/ppermute | solution.py:163
  12.4 0.2 collective-permute-start.8
  12.6 0.2 collective-permute-start.9
  12.8 1.2 %collective-permute-start = (bf16[2,128,256]{2,1,0:T(8,128)(2,1)S(1)}, bf16[2,128,256]{2,1,0:T(8,128)(2,1)S(1)}, u32[]{:S(2)}, u32[]{:S(2)}) collective-permute-start(bf16[2,128,256]{2,1,0:T(8,128)(2,1)S(1)} %get-tuple-element.16), channel_id=1, source_target_pairs={{0,1},{1,0},{2,3},{3,2},{4,5},{5,4},{6,7},{7,6},{8,9},{9,8},{10,11... | collective-permute-start | bytes 393224 | tf_op jit(solution)/shard_map/ppermute | solution.py:163
  14.0 1.3 %collective-permute-start.1 = (bf16[2,128,256]{2,1,0:T(8,128)(2,1)S(1)}, bf16[2,128,256]{2,1,0:T(8,128)(2,1)S(1)}, u32[]{:S(2)}, u32[]{:S(2)}) collective-permute-start(bf16[2,128,256]{2,1,0:T(8,128)(2,1)S(1)} %get-tuple-element.17), channel_id=1, source_target_pairs={{0,2},{1,3},{2,0},{3,1},{4,6},{5,7},{6,4},{7,5},{8,10},{9,11},{10,... | collective-permute-start | bytes 393224 | tf_op jit(solution)/shard_map/ppermute | solution.py:163
  15.3 0.0 copy-done
  15.4 0.0 copy-done.1
  15.4 0.0 copy-done.2
  15.4 0.0 copy-done.3
  15.4 0.4 select_reduce_fusion
  15.9 0.0 collective-permute-done.10
  15.9 1.9 %collective-permute-start.2 = (bf16[2,128,256]{2,1,0:T(8,128)(2,1)S(1)}, bf16[2,128,256]{2,1,0:T(8,128)(2,1)S(1)}, u32[]{:S(2)}, u32[]{:S(2)}) collective-permute-start(bf16[2,128,256]{2,1,0:T(8,128)(2,1)S(1)} %get-tuple-element.18), channel_id=1, source_target_pairs={{0,3},{1,2},{2,1},{3,0},{4,7},{5,6},{6,5},{7,4},{8,11},{9,10},{10,... | collective-permute-start | bytes 393224 | tf_op jit(solution)/shard_map/ppermute | solution.py:163
  17.8 1.4 %collective-permute-done.8 = bf16[2,128,256]{2,1,0:T(8,128)(2,1)S(1)} collective-permute-done((bf16[2,128,256]{2,1,0:T(8,128)(2,1)S(1)}, bf16[2,128,256]{2,1,0:T(8,128)(2,1)S(1)}, u32[]{:S(2)}, u32[]{:S(2)}) %collective-permute-start.8) | collective-permute-done | bytes 131104 | tf_op jit(solution)/shard_map/ppermute | solution.py:163
  19.2 0.0 collective-permute-done.9
  19.2 0.1 fusion.12
  19.2 2.4 %collective-permute-start.11 = (bf16[2,128,256]{2,1,0:T(8,128)(2,1)S(1)}, bf16[2,128,256]{2,1,0:T(8,128)(2,1)S(1)}, u32[]{:S(2)}, u32[]{:S(2)}) collective-permute-start(bf16[2,128,256]{2,1,0:T(8,128)(2,1)S(1)} %fusion.12), channel_id=1, source_target_pairs={{0,4},{1,5},{2,6},{3,7},{4,0},{5,1},{6,2},{7,3},{8,12},{9,13},{10,... | collective-permute-start | bytes 393224 | tf_op jit(solution)/shard_map/ppermute | solution.py:166
  21.7 1.7 %collective-permute-done = bf16[2,128,256]{2,1,0:T(8,128)(2,1)S(1)} collective-permute-done((bf16[2,128,256]{2,1,0:T(8,128)(2,1)S(1)}, bf16[2,128,256]{2,1,0:T(8,128)(2,1)S(1)}, u32[]{:S(2)}, u32[]{:S(2)}) %collective-permute-start) | collective-permute-done | bytes 131104 | tf_op jit(solution)/shard_map/ppermute | solution.py:163
  23.4 0.0 collective-permute-done.1
  23.4 0.0 collective-permute-done.2
  23.4 0.1 fusion.11
  23.5 3.4 %collective-permute-start.3 = (bf16[2,128,256]{2,1,0:T(8,128)(2,1)S(1)}, bf16[2,128,256]{2,1,0:T(8,128)(2,1)S(1)}, u32[]{:S(2)}, u32[]{:S(2)}) collective-permute-start(bf16[2,128,256]{2,1,0:T(8,128)(2,1)S(1)} %fusion.11), channel_id=1, source_target_pairs={{0,4},{1,5},{2,6},{3,7},{4,0},{5,1},{6,2},{7,3},{8,12},{9,13},{10,... | collective-permute-start | bytes 393224 | tf_op jit(solution)/shard_map/ppermute | solution.py:166
  26.8 0.0 collective-permute-done.11
  26.8 0.1 add_convert_fusion
  26.9 1.3 %collective-permute-start.12 = (bf16[272,256]{1,0:T(8,128)(2,1)S(1)}, bf16[272,256]{1,0:T(8,128)(2,1)S(1)}, u32[]{:S(2)}, u32[]{:S(2)}) collective-permute-start(bf16[272,256]{1,0:T(8,128)(2,1)S(1)} %pad_maximum_fusion.5), channel_id=1, source_target_pairs={{0,16},{8,24},{16,0},{24,8},{1,17},{9,25},{17,1},{25,9},{2,18},{10... | collective-permute-start | bytes 417800 | tf_op jit(solution)/shard_map/ppermute | solution.py:179
  28.2 6.5 %collective-permute-done.3 = bf16[2,128,256]{2,1,0:T(8,128)(2,1)S(1)} collective-permute-done((bf16[2,128,256]{2,1,0:T(8,128)(2,1)S(1)}, bf16[2,128,256]{2,1,0:T(8,128)(2,1)S(1)}, u32[]{:S(2)}, u32[]{:S(2)}) %collective-permute-start.3) | collective-permute-done | bytes 131104 | tf_op jit(solution)/shard_map/ppermute | solution.py:166
  34.7 0.1 add_convert_fusion.1
  34.8 0.0 collective-permute-done.12
  34.8 1.2 %collective-permute-start.13 = (bf16[272,512]{1,0:T(8,128)(2,1)S(1)}, bf16[272,512]{1,0:T(8,128)(2,1)S(1)}, u32[]{:S(2)}, u32[]{:S(2)}) collective-permute-start(bf16[272,512]{1,0:T(8,128)(2,1)S(1)} %pad_maximum_fusion.3), channel_id=1, source_target_pairs={{0,8},{8,0},{16,24},{24,16},{1,9},{9,1},{17,25},{25,17},{2,10},{10... | collective-permute-start | bytes 835592 | tf_op jit(solution)/shard_map/ppermute | solution.py:181
  36.0 1.3 %collective-permute-start.4 = (bf16[272,256]{1,0:T(8,128)(2,1)S(1)}, bf16[272,256]{1,0:T(8,128)(2,1)S(1)}, u32[]{:S(2)}, u32[]{:S(2)}) collective-permute-start(bf16[272,256]{1,0:T(8,128)(2,1)S(1)} %pad_maximum_fusion.4), channel_id=1, source_target_pairs={{0,16},{8,24},{16,0},{24,8},{1,17},{9,25},{17,1},{25,9},{2,18},{10... | collective-permute-start | bytes 417800 | tf_op jit(solution)/shard_map/ppermute | solution.py:179
  37.3 0.0 copy-done.4
  37.3 4.0 %collective-permute-done.4 = bf16[272,256]{1,0:T(8,128)(2,1)S(1)} collective-permute-done((bf16[272,256]{1,0:T(8,128)(2,1)S(1)}, bf16[272,256]{1,0:T(8,128)(2,1)S(1)}, u32[]{:S(2)}, u32[]{:S(2)}) %collective-permute-start.4) | collective-permute-done | bytes 139296 | tf_op jit(solution)/shard_map/ppermute | solution.py:179
  41.3 0.9 %collective-permute-start.5 = (bf16[272,512]{1,0:T(8,128)(2,1)S(1)}, bf16[272,512]{1,0:T(8,128)(2,1)S(1)}, u32[]{:S(2)}, u32[]{:S(2)}) collective-permute-start(bf16[272,512]{1,0:T(8,128)(2,1)S(1)} %pad_maximum_fusion.2), channel_id=1, source_target_pairs={{0,8},{8,0},{16,24},{24,16},{1,9},{9,1},{17,25},{25,17},{2,10},{10... | collective-permute-start | bytes 835592 | tf_op jit(solution)/shard_map/ppermute | solution.py:181
  42.3 0.0 collective-permute-done.13
  42.3 0.1 broadcast_select_fusion.1
  42.4 0.1 pad_maximum_fusion
  42.4 0.1 dynamic-slice_bitcast_fusion
  42.5 1.0 %collective-permute-start.14 = (bf16[128,1024]{1,0:T(8,128)(2,1)S(1)}, bf16[128,1024]{1,0:T(8,128)(2,1)S(1)}, u32[]{:S(2)}, u32[]{:S(2)}) collective-permute-start(bf16[128,1024]{1,0:T(8,128)(2,1)S(1)} %get-tuple-element.37), channel_id=1, source_target_pairs={{0,1},{1,0},{2,8},{3,9},{4,5},{5,4},{6,12},{7,13},{8,2},{9,3},{10,... | collective-permute-start | bytes 786440 | tf_op jit(solution)/shard_map/ppermute | solution.py:195
  43.5 0.8 %collective-permute-start.15 = (bf16[128,1024]{1,0:T(8,128)(2,1)S(1)}, bf16[128,1024]{1,0:T(8,128)(2,1)S(1)}, u32[]{:S(2)}, u32[]{:S(2)}) collective-permute-start(bf16[128,1024]{1,0:T(8,128)(2,1)S(1)} %get-tuple-element.37), channel_id=1, source_target_pairs={{0,3},{1,2},{2,10},{3,11},{4,7},{5,6},{6,14},{7,15},{8,0},{9,1},{1... | collective-permute-start | bytes 786440 | tf_op jit(solution)/shard_map/ppermute | solution.py:196
  44.2 0.0 collective-permute-done.5
  44.2 0.1 broadcast_select_fusion.3
  44.3 0.1 pad_maximum_fusion.1
  44.4 0.1 dynamic-slice_bitcast_fusion.1
  44.5 0.7 %collective-permute-start.6 = (bf16[128,1024]{1,0:T(8,128)(2,1)S(1)}, bf16[128,1024]{1,0:T(8,128)(2,1)S(1)}, u32[]{:S(2)}, u32[]{:S(2)}) collective-permute-start(bf16[128,1024]{1,0:T(8,128)(2,1)S(1)} %get-tuple-element.39), channel_id=1, source_target_pairs={{0,1},{1,0},{2,8},{3,9},{4,5},{5,4},{6,12},{7,13},{8,2},{9,3},{10,... | collective-permute-start | bytes 786440 | tf_op jit(solution)/shard_map/ppermute | solution.py:195
  45.2 1.3 %collective-permute-start.7 = (bf16[128,1024]{1,0:T(8,128)(2,1)S(1)}, bf16[128,1024]{1,0:T(8,128)(2,1)S(1)}, u32[]{:S(2)}, u32[]{:S(2)}) collective-permute-start(bf16[128,1024]{1,0:T(8,128)(2,1)S(1)} %get-tuple-element.39), channel_id=1, source_target_pairs={{0,3},{1,2},{2,10},{3,11},{4,7},{5,6},{6,14},{7,15},{8,0},{9,1},{1... | collective-permute-start | bytes 786440 | tf_op jit(solution)/shard_map/ppermute | solution.py:196
  46.6 0.1 divide_multiply_fusion
  46.7 9.2 %collective-permute-done.6 = bf16[128,1024]{1,0:T(8,128)(2,1)S(1)} collective-permute-done((bf16[128,1024]{1,0:T(8,128)(2,1)S(1)}, bf16[128,1024]{1,0:T(8,128)(2,1)S(1)}, u32[]{:S(2)}, u32[]{:S(2)}) %collective-permute-start.6) | collective-permute-done | bytes 262176 | tf_op jit(solution)/shard_map/ppermute | solution.py:195
  55.8 2.0 %collective-permute-done.7 = bf16[128,1024]{1,0:T(8,128)(2,1)S(1)} collective-permute-done((bf16[128,1024]{1,0:T(8,128)(2,1)S(1)}, bf16[128,1024]{1,0:T(8,128)(2,1)S(1)}, u32[]{:S(2)}, u32[]{:S(2)}) %collective-permute-start.7) | collective-permute-done | bytes 262176 | tf_op jit(solution)/shard_map/ppermute | solution.py:196
  57.9 0.8 %fusion = f32[8,128,256]{2,1,0:T(8,128)S(1)} fusion(f32[128,1024]{1,0:T(8,128)S(1)} %get-tuple-element.40, f32[8,1024]{1,0:T(8,128)S(1)} %get-tuple-element.48, bf16[128,1024]{1,0:T(8,128)(2,1)S(1)} %get-tuple-element.32, bf16[128,1024]{1,0:T(8,128)(2,1)S(1)} %get-tuple-element.31), kind=kOutput, calls=%fused_computation.2 | convolution fusion | flops 540016640 | bytes 2129920 | tf_op jit(solution)/shard_map/kpc,nc->kpn/dot_general | solution.py:254
  58.7 0.0 collective-permute-done.14
  58.7 0.0 collective-permute-done.15
  58.7 0.1 broadcast_select_fusion.9
  58.8 1.7 %fusion.6 = f32[8,128,256]{2,1,0:T(8,128)} fusion(f32[8,128,256]{2,1,0:T(8,128)S(1)} %fusion, f32[128,1024]{1,0:T(8,128)S(1)} %get-tuple-element.38, f32[8,1024]{1,0:T(8,128)S(1)} %get-tuple-element.47, bf16[128,1024]{1,0:T(8,128)(2,1)S(1)} %get-tuple-element.30, bf16[128,1024]{1,0:T(8,128)(2,1)S(1)} %get-tuple-element.29), kind=kOutput, calls=%fused_computation.8 | convolution fusion | flops 540278784 | bytes 3178496 | tf_op jit(solution)/shard_map/kpc,nc->kpn/dot_general | solution.py:254
  (20 shorter events, 0.2 us)
Async XLA Ops:
  6.6 8.7 %copy-start = (s32[512]{0:T(512)S(1)}, s32[512]{0:T(512)}, u32[]{:S(2)}) copy-start(s32[512]{0:T(512)} %param.12) | copy-start | bytes 6148
  6.6 8.7 %copy-start.1 = (s32[512]{0:T(512)S(1)}, s32[512]{0:T(512)}, u32[]{:S(2)}) copy-start(s32[512]{0:T(512)} %param.13) | copy-start | bytes 6148
  6.6 8.7 %copy-start.2 = (f32[128]{0:T(128)S(1)}, f32[128]{0:T(128)}, u32[]{:S(2)}) copy-start(f32[128]{0:T(128)} %param.9) | copy-start | bytes 1540
  6.7 8.7 %copy-start.3 = (f32[128]{0:T(128)S(1)}, f32[128]{0:T(128)}, u32[]{:S(2)}) copy-start(f32[128]{0:T(128)} %param.10) | copy-start | bytes 1540
  9.2 28.1 %copy-start.4 = (f32[8]{0:T(128)S(1)}, f32[8]{0:T(128)}, u32[]{:S(2)}) copy-start(f32[8]{0:T(128)} %param.11) | copy-start | bytes 100
  9.2 6.6 %collective-permute-start.10 = (bf16[2,128,256]{2,1,0:T(8,128)(2,1)S(1)}, bf16[2,128,256]{2,1,0:T(8,128)(2,1)S(1)}, u32[]{:S(2)}, u32[]{:S(2)}) collective-permute-start(bf16[2,128,256]{2,1,0:T(8,128)(2,1)S(1)} %get-tuple-element.24), channel_id=1, source_target_pairs={{0,3},{1,2},{2,1},{3,0},{4,7},{5,6},{6,5},{7,4},{8,11},{9,10},{10,... | collective-permute-start | bytes 393224 | tf_op jit(solution)/shard_map/ppermute | solution.py:163
  12.4 6.7 %collective-permute-start.8 = (bf16[2,128,256]{2,1,0:T(8,128)(2,1)S(1)}, bf16[2,128,256]{2,1,0:T(8,128)(2,1)S(1)}, u32[]{:S(2)}, u32[]{:S(2)}) collective-permute-start(bf16[2,128,256]{2,1,0:T(8,128)(2,1)S(1)} %get-tuple-element.22), channel_id=1, source_target_pairs={{0,1},{1,0},{2,3},{3,2},{4,5},{5,4},{6,7},{7,6},{8,9},{9,8},{10,11... | collective-permute-start | bytes 393224 | tf_op jit(solution)/shard_map/ppermute | solution.py:163
  12.6 6.6 %collective-permute-start.9 = (bf16[2,128,256]{2,1,0:T(8,128)(2,1)S(1)}, bf16[2,128,256]{2,1,0:T(8,128)(2,1)S(1)}, u32[]{:S(2)}, u32[]{:S(2)}) collective-permute-start(bf16[2,128,256]{2,1,0:T(8,128)(2,1)S(1)} %get-tuple-element.23), channel_id=1, source_target_pairs={{0,2},{1,3},{2,0},{3,1},{4,6},{5,7},{6,4},{7,5},{8,10},{9,11},{10,... | collective-permute-start | bytes 393224 | tf_op jit(solution)/shard_map/ppermute | solution.py:163
  12.8 10.6 %collective-permute-start = (bf16[2,128,256]{2,1,0:T(8,128)(2,1)S(1)}, bf16[2,128,256]{2,1,0:T(8,128)(2,1)S(1)}, u32[]{:S(2)}, u32[]{:S(2)}) collective-permute-start(bf16[2,128,256]{2,1,0:T(8,128)(2,1)S(1)} %get-tuple-element.16), channel_id=1, source_target_pairs={{0,1},{1,0},{2,3},{3,2},{4,5},{5,4},{6,7},{7,6},{8,9},{9,8},{10,11... | collective-permute-start | bytes 393224 | tf_op jit(solution)/shard_map/ppermute | solution.py:163
  14.0 9.4 %collective-permute-start.1 = (bf16[2,128,256]{2,1,0:T(8,128)(2,1)S(1)}, bf16[2,128,256]{2,1,0:T(8,128)(2,1)S(1)}, u32[]{:S(2)}, u32[]{:S(2)}) collective-permute-start(bf16[2,128,256]{2,1,0:T(8,128)(2,1)S(1)} %get-tuple-element.17), channel_id=1, source_target_pairs={{0,2},{1,3},{2,0},{3,1},{4,6},{5,7},{6,4},{7,5},{8,10},{9,11},{10,... | collective-permute-start | bytes 393224 | tf_op jit(solution)/shard_map/ppermute | solution.py:163
  15.9 7.5 %collective-permute-start.2 = (bf16[2,128,256]{2,1,0:T(8,128)(2,1)S(1)}, bf16[2,128,256]{2,1,0:T(8,128)(2,1)S(1)}, u32[]{:S(2)}, u32[]{:S(2)}) collective-permute-start(bf16[2,128,256]{2,1,0:T(8,128)(2,1)S(1)} %get-tuple-element.18), channel_id=1, source_target_pairs={{0,3},{1,2},{2,1},{3,0},{4,7},{5,6},{6,5},{7,4},{8,11},{9,10},{10,... | collective-permute-start | bytes 393224 | tf_op jit(solution)/shard_map/ppermute | solution.py:163
  19.2 7.6 %collective-permute-start.11 = (bf16[2,128,256]{2,1,0:T(8,128)(2,1)S(1)}, bf16[2,128,256]{2,1,0:T(8,128)(2,1)S(1)}, u32[]{:S(2)}, u32[]{:S(2)}) collective-permute-start(bf16[2,128,256]{2,1,0:T(8,128)(2,1)S(1)} %fusion.12), channel_id=1, source_target_pairs={{0,4},{1,5},{2,6},{3,7},{4,0},{5,1},{6,2},{7,3},{8,12},{9,13},{10,... | collective-permute-start | bytes 393224 | tf_op jit(solution)/shard_map/ppermute | solution.py:166
  23.5 11.2 %collective-permute-start.3 = (bf16[2,128,256]{2,1,0:T(8,128)(2,1)S(1)}, bf16[2,128,256]{2,1,0:T(8,128)(2,1)S(1)}, u32[]{:S(2)}, u32[]{:S(2)}) collective-permute-start(bf16[2,128,256]{2,1,0:T(8,128)(2,1)S(1)} %fusion.11), channel_id=1, source_target_pairs={{0,4},{1,5},{2,6},{3,7},{4,0},{5,1},{6,2},{7,3},{8,12},{9,13},{10,... | collective-permute-start | bytes 393224 | tf_op jit(solution)/shard_map/ppermute | solution.py:166
  26.9 7.8 %collective-permute-start.12 = (bf16[272,256]{1,0:T(8,128)(2,1)S(1)}, bf16[272,256]{1,0:T(8,128)(2,1)S(1)}, u32[]{:S(2)}, u32[]{:S(2)}) collective-permute-start(bf16[272,256]{1,0:T(8,128)(2,1)S(1)} %pad_maximum_fusion.5), channel_id=1, source_target_pairs={{0,16},{8,24},{16,0},{24,8},{1,17},{9,25},{17,1},{25,9},{2,18},{10... | collective-permute-start | bytes 417800 | tf_op jit(solution)/shard_map/ppermute | solution.py:179
  34.8 7.5 %collective-permute-start.13 = (bf16[272,512]{1,0:T(8,128)(2,1)S(1)}, bf16[272,512]{1,0:T(8,128)(2,1)S(1)}, u32[]{:S(2)}, u32[]{:S(2)}) collective-permute-start(bf16[272,512]{1,0:T(8,128)(2,1)S(1)} %pad_maximum_fusion.3), channel_id=1, source_target_pairs={{0,8},{8,0},{16,24},{24,16},{1,9},{9,1},{17,25},{25,17},{2,10},{10... | collective-permute-start | bytes 835592 | tf_op jit(solution)/shard_map/ppermute | solution.py:181
  36.0 5.3 %collective-permute-start.4 = (bf16[272,256]{1,0:T(8,128)(2,1)S(1)}, bf16[272,256]{1,0:T(8,128)(2,1)S(1)}, u32[]{:S(2)}, u32[]{:S(2)}) collective-permute-start(bf16[272,256]{1,0:T(8,128)(2,1)S(1)} %pad_maximum_fusion.4), channel_id=1, source_target_pairs={{0,16},{8,24},{16,0},{24,8},{1,17},{9,25},{17,1},{25,9},{2,18},{10... | collective-permute-start | bytes 417800 | tf_op jit(solution)/shard_map/ppermute | solution.py:179
  41.3 2.9 %collective-permute-start.5 = (bf16[272,512]{1,0:T(8,128)(2,1)S(1)}, bf16[272,512]{1,0:T(8,128)(2,1)S(1)}, u32[]{:S(2)}, u32[]{:S(2)}) collective-permute-start(bf16[272,512]{1,0:T(8,128)(2,1)S(1)} %pad_maximum_fusion.2), channel_id=1, source_target_pairs={{0,8},{8,0},{16,24},{24,16},{1,9},{9,1},{17,25},{25,17},{2,10},{10... | collective-permute-start | bytes 835592 | tf_op jit(solution)/shard_map/ppermute | solution.py:181
  42.5 16.2 %collective-permute-start.14 = (bf16[128,1024]{1,0:T(8,128)(2,1)S(1)}, bf16[128,1024]{1,0:T(8,128)(2,1)S(1)}, u32[]{:S(2)}, u32[]{:S(2)}) collective-permute-start(bf16[128,1024]{1,0:T(8,128)(2,1)S(1)} %get-tuple-element.37), channel_id=1, source_target_pairs={{0,1},{1,0},{2,8},{3,9},{4,5},{5,4},{6,12},{7,13},{8,2},{9,3},{10,... | collective-permute-start | bytes 786440 | tf_op jit(solution)/shard_map/ppermute | solution.py:195
  43.5 15.2 %collective-permute-start.15 = (bf16[128,1024]{1,0:T(8,128)(2,1)S(1)}, bf16[128,1024]{1,0:T(8,128)(2,1)S(1)}, u32[]{:S(2)}, u32[]{:S(2)}) collective-permute-start(bf16[128,1024]{1,0:T(8,128)(2,1)S(1)} %get-tuple-element.37), channel_id=1, source_target_pairs={{0,3},{1,2},{2,10},{3,11},{4,7},{5,6},{6,14},{7,15},{8,0},{9,1},{1... | collective-permute-start | bytes 786440 | tf_op jit(solution)/shard_map/ppermute | solution.py:196
  44.5 11.3 %collective-permute-start.6 = (bf16[128,1024]{1,0:T(8,128)(2,1)S(1)}, bf16[128,1024]{1,0:T(8,128)(2,1)S(1)}, u32[]{:S(2)}, u32[]{:S(2)}) collective-permute-start(bf16[128,1024]{1,0:T(8,128)(2,1)S(1)} %get-tuple-element.39), channel_id=1, source_target_pairs={{0,1},{1,0},{2,8},{3,9},{4,5},{5,4},{6,12},{7,13},{8,2},{9,3},{10,... | collective-permute-start | bytes 786440 | tf_op jit(solution)/shard_map/ppermute | solution.py:195
  45.2 12.7 %collective-permute-start.7 = (bf16[128,1024]{1,0:T(8,128)(2,1)S(1)}, bf16[128,1024]{1,0:T(8,128)(2,1)S(1)}, u32[]{:S(2)}, u32[]{:S(2)}) collective-permute-start(bf16[128,1024]{1,0:T(8,128)(2,1)S(1)} %get-tuple-element.39), channel_id=1, source_target_pairs={{0,3},{1,2},{2,10},{3,11},{4,7},{5,6},{6,14},{7,15},{8,0},{9,1},{1... | collective-permute-start | bytes 786440 | tf_op jit(solution)/shard_map/ppermute | solution.py:196
